TPU v7x, 512 devices: a whole 4x8x8 slice. The times are simulated.
512 devices in a mesh: vocab: 128 (over y_lo, z, x, core), seq: 4 (over y_hi).
Axes of the slice: x: 4, y: 8 (y_hi: 4, y_lo: 2; y = y_hi * 2 + y_lo), z: 8, core: 2. Of those that a mesh axis runs over, the one named last changes fastest.
Arguments:
- latent_vector: bfloat16 [512, 7168], P('vocab', 'seq'), may hold values from -400 to 400
- unembedding_matrix: bfloat16 [7168, 131072], P('seq', 'vocab'), may hold values from -0.0625 to 0.0625
- occurrence_tally: int32 [512, 131072], P(('seq', 'vocab')), may hold values from 0 to 2
- additive_offset_table: bfloat16 [512, 131072], P(('seq', 'vocab')), may hold values from 0 to 0.5
- recurrence_charge: float32 [512], P(('seq', 'vocab')), may hold values from 0.05 to 0.5
- appearance_charge: float32 [512], P(('seq', 'vocab')), may hold values from 0.6 to 1.5
- recurrence_divisor: float32 [512], P('seq'), may hold values from 1.05 to 1.6
- softening_divisor: float32 [512], P('seq'), may hold values from 0.5 to 1.5
- nucleus_share_limit: float32 [512], P('seq'), may hold values from 0.5 to 0.95
Outputs:
- penalized_logits: bfloat16 [512, 131072], P('seq', 'vocab')
- cutoff: float32 [512], P('seq')
Inputs may be any that keep to these rules, and one draw needn't show every extreme that they name: `appearance_charge`: each sequence's presence penalty exceeds every entry of its token bias.
All inputs are finite; a program needn't handle non-finite values.
Results may differ from a plain program's by a relative error of at most 0.0047.
Values may be sent and summed in bfloat16 or wider, within the bound.
A program may use at most 64 MiB of HBM per device.

v0:
```python
import jax
import jax.numpy as jnp
from jax import lax
from jax.sharding import Mesh
from jax.sharding import PartitionSpec as P

STEPS = 9
VOCAB = ("vocab_0", "vocab_1", "vocab_2", "vocab_3")
SEQ_VOCAB = ("seq", "vocab_0", "vocab_1", "vocab_2", "vocab_3")


cutoff_span = 32.0


def sent_to_all(array, axis):
    count = lax.axis_size(axis)
    return lax.all_to_all(
        jnp.broadcast_to(array[None], (count, *array.shape)), axis, 0, 0, tiled=True
    )


def in_order(tiles, dim):
    lengths = list(tiles.shape[1:])
    lengths[dim] *= tiles.shape[0]
    return jnp.moveaxis(tiles, 0, dim).reshape(lengths)


def gather_axes(array, axes, dim):
    far, near = axes
    first = sent_to_all(array, far)
    tiles = jnp.swapaxes(sent_to_all(first, near), 0, 1)
    return in_order(tiles.reshape(-1, *array.shape), dim)


def split_up(array, dim, count):
    lengths = array.shape
    tiles = array.reshape(*lengths[:dim], count, lengths[dim] // count, *lengths[dim + 1 :])
    return jnp.moveaxis(tiles, dim, 0)


def sum_at_owner(array, axis, dim):
    tiles = split_up(array, dim, lax.axis_size(axis))
    arrived = lax.all_to_all(tiles, axis, split_axis=0, concat_axis=0, tiled=True)
    return arrived.sum(axis=0)


def gathered_once(array, axis):
    leaves = jax.tree.leaves(array)
    sequence = sorted(range(len(leaves)), key=lambda k: -leaves[k].size)
    width = (1, *leaves[sequence[0]].shape)[-1]
    lines = [
        jnp.pad(leaves[k].reshape(-1), (0, -leaves[k].size % width)).reshape(-1, width)
        for k in sequence
    ]
    both, at, found = (lax.all_gather(jnp.concatenate(lines), axis), 0, {})
    for k, line in zip(sequence, lines):
        share = both[:, at : at + len(line)].reshape(len(both), -1)
        found[k] = share[:, : leaves[k].size].reshape(-1, *leaves[k].shape)
        at += len(line)
    numbers = iter(range(len(leaves)))
    return jax.tree.map(lambda _: found[next(numbers)], array)


def joined_all(array, axes, combine):
    for axis in axes:
        pieces = gathered_once(array, axis)
        array = jax.tree.map(lambda part: part[0], pieces)
        for k in range(1, lax.axis_size(axis)):
            array = combine(array, jax.tree.map(lambda part: part[k], pieces))
    return array


def taken_together(array, axis):
    everything = sent_to_all(array, axis)
    return jnp.sum(everything, axis=0)


def by_axis(array, axes):
    far, near = axes
    nearer = taken_together(array, near)
    return taken_together(nearer, far)


def per_device(
    latent_vector,
    unembedding_matrix,
    occurrence_tally,
    additive_offset_table,
    recurrence_charge,
    appearance_charge,
    recurrence_divisor,
    softening_divisor,
    nucleus_share_limit,
):
    count_float = occurrence_tally.astype(jnp.float32)
    offset = (
        additive_offset_table.astype(jnp.float32)
        - recurrence_charge[:, None] * count_float
        - appearance_charge[:, None] * (occurrence_tally > 0).astype(jnp.float32)
    ).astype(jnp.bfloat16)
    relaid = lax.all_to_all(offset, VOCAB, split_axis=1, concat_axis=0, tiled=True)
    partial_logits = jnp.dot(
        gather_axes(latent_vector, (("vocab_0", "vocab_1", "vocab_2"), "vocab_3"), 0),
        unembedding_matrix,
        preferred_element_type=jnp.float32,
    )
    logits = sum_at_owner(partial_logits, "seq", 0)
    seen_mask = relaid < 0
    factor = recurrence_divisor[:, None]
    discouraged_scores = jnp.where(
        seen_mask, jnp.where(logits > 0, logits / factor, logits * factor), logits
    ) + relaid.astype(jnp.float32)
    softened_scores = discouraged_scores / softening_divisor[:, None]
    local_max = jnp.max(softened_scores, axis=1)
    local_total = jnp.sum(jnp.exp(softened_scores - local_max[:, None]), axis=1)

    def combine(former, latter):
        largest = jnp.maximum(former[0], latter[0])
        return (
            largest,
            former[1] * jnp.exp(former[0] - largest) + latter[1] * jnp.exp(latter[0] - largest),
        )

    largest_score, row_total = joined_all((local_max, local_total), VOCAB, combine)
    exponential_values = jnp.exp(softened_scores - largest_score[:, None])
    target = nucleus_share_limit * row_total
    start_bounds = (jnp.zeros_like(largest_score), jnp.ones_like(largest_score))
    fractions = jnp.arange(1, 8, dtype=jnp.float32)

    def refine(turn_index, bounds):
        lower_end, upper_end = bounds
        stride = (upper_end - lower_end) * 0.125
        probes = lower_end[:, None] + stride[:, None] * fractions[None, :]
        threshold_candidates = largest_score[:, None] - cutoff_span * probes
        inside = softened_scores[:, None, :] >= threshold_candidates[:, :, None]
        partial_mass = jnp.sum(jnp.where(inside, exponential_values[:, None, :], 0.0), axis=2)
        cumulative_shares = by_axis(partial_mass, (("vocab_0", "vocab_1"), ("vocab_2", "vocab_3")))
        below_count = jnp.sum((cumulative_shares < target[:, None]).astype(jnp.float32), axis=1)
        new_lower = lower_end + stride * below_count
        return (new_lower, new_lower + stride)

    lower_end, upper_end = lax.fori_loop(0, STEPS // 3, refine, start_bounds)
    return (discouraged_scores.astype(jnp.bfloat16), largest_score - cutoff_span * upper_end)


def solution(mesh):
    split = Mesh(
        mesh.devices.reshape(2, 8, 4, 2, mesh.shape["seq"]),
        ("vocab_0", "vocab_1", "vocab_2", "vocab_3", "seq"),
    )
    placed = (
        P(VOCAB, "seq"),
        P("seq", VOCAB),
        P(SEQ_VOCAB, None),
        P(SEQ_VOCAB, None),
        P(SEQ_VOCAB),
        P(SEQ_VOCAB),
        P("seq"),
        P("seq"),
        P("seq"),
    )
    return jax.shard_map(
        per_device,
        mesh=split,
        in_specs=placed,
        out_specs=(P("seq", VOCAB), P("seq")),
        check_vma=False,
    )
```

profile of v0, /device:TPU:1, one launch (start us, length us, event | category | flops | bytes accessed | tf_op | source)
XLA Modules:
  0.0 226.3 jit_solution(17373440366717739609)
XLA Ops:
  3.9 15.3 %all-to-all-start.3 = ((bf16[64,4,1792]{2,1,0:T(4,128)(2,1)}), bf16[64,4,1792]{2,1,0:T(4,128)(2,1)S(1)}, u32[]{:S(2)}, u32[]{:S(2)}) async-start(bf16[64,4,1792]{2,1,0:T(4,128)(2,1)} %broadcast_in_dim.20), calls=%async_computation.3 | async-start | bytes 1835008 | tf_op jit(solution)/shard_map/all_to_all | solution.py:17
  20.9 2.1 reduce
  23.9 16.4 %all-to-all-done.3 = bf16[64,4,1792]{2,1,0:T(4,128)(2,1)S(1)} async-done(((bf16[64,4,1792]{2,1,0:T(4,128)(2,1)}), bf16[64,4,1792]{2,1,0:T(4,128)(2,1)S(1)}, u32[]{:S(2)}, u32[]{:S(2)}) %all-to-all-start.3) | async-done | bytes 917536 | tf_op jit(solution)/shard_map/all_to_all | solution.py:17
  40.8 8.9 %all_to_all.42 = bf16[2,64,4,1792]{3,2,1,0:T(4,128)(2,1)S(1)} all-to-all(bf16[2,64,4,1792]{3,2,1,0:T(4,128)(2,1)S(1)} %broadcast_in_dim.21), channel_id=1, replica_groups=mesh['vocab_0'=2,'vocab_1'=8,'vocab_2'=4,'vocab_3'=2,'seq'=4] {'vocab_3'}, dimensions={0} | all-to-all | bytes 3670016 | tf_op jit(solution)/shard_map/all_to_all | solution.py:17
  51.8 8.4 %all-to-all-start.2 = ((bf16[128,2,512]{2,1,0:T(2,128)(2,1)}), bf16[128,2,512]{2,1,0:T(2,128)(2,1)S(1)}, u32[]{:S(2)}, u32[]{:S(2)}) async-start(bf16[128,2,512]{2,1,0:T(2,128)(2,1)} %reshape.815), calls=%async_computation.2 | async-start | bytes 524288 | tf_op jit(solution)/shard_map/all_to_all | solution.py:101
  60.2 6.0 %fusion.4 = f32[4,128,1024]{2,1,0:T(8,128)} fusion(bf16[4,128,1792]{2,1,0:T(8,128)(2,1)} %dot_general.5, bf16[1792,1024]{1,0:T(8,128)(2,1)} %param.12), kind=kOutput, calls=%fused_computation.10 | convolution fusion | flops 1879048192 | bytes 7602176 | tf_op jit(solution)/shard_map/dot_general | solution.py:102
  66.2 7.5 %all-to-all-done.2 = bf16[128,2,512]{2,1,0:T(2,128)(2,1)S(1)} async-done(((bf16[128,2,512]{2,1,0:T(2,128)(2,1)}), bf16[128,2,512]{2,1,0:T(2,128)(2,1)S(1)}, u32[]{:S(2)}, u32[]{:S(2)}) %all-to-all-start.2) | async-done | bytes 262176 | tf_op jit(solution)/shard_map/all_to_all | solution.py:101
  73.7 5.9 %all-to-all-start.5 = ((f32[4,128,1024]{2,1,0:T(8,128)}), f32[4,128,1024]{2,1,0:T(8,128)S(1)}, u32[]{:S(2)}, u32[]{:S(2)}) async-start(f32[4,128,1024]{2,1,0:T(8,128)} %fusion.4), calls=%async_computation.5 | async-start | bytes 4194304 | tf_op jit(solution)/shard_map/all_to_all | solution.py:43
  80.5 32.2 %all-to-all-done.5 = f32[4,128,1024]{2,1,0:T(8,128)S(1)} async-done(((f32[4,128,1024]{2,1,0:T(8,128)}), f32[4,128,1024]{2,1,0:T(8,128)S(1)}, u32[]{:S(2)}, u32[]{:S(2)}) %all-to-all-start.5) | async-done | bytes 2097184 | tf_op jit(solution)/shard_map/all_to_all | solution.py:43
  113.7 2.1 fusion.62
  116.0 19.5 %all-gather.4 = f32[2,2,128]{2,1,0:T(2,128)S(1)} all-gather(f32[1,2,128]{2,1,0:T(2,128)S(1)} %maximum_bitcast_fusion), channel_id=2, replica_groups=mesh['vocab_0'=2,'vocab_1'=8,'vocab_2'=4,'vocab_3'=2,'seq'=4] {'vocab_0'}, dimensions={0}, use_global_device_ids=true | all-gather | bytes 3072 | tf_op jit(solution)/shard_map/all_gather | solution.py:55
  135.5 10.4 %all-gather.5 = f32[8,2,128]{2,1,0:T(2,128)S(1)} all-gather(f32[1,2,128]{2,1,0:T(2,128)S(1)} %maximum_bitcast_fusion.1), channel_id=3, replica_groups=mesh['vocab_0'=2,'vocab_1'=8,'vocab_2'=4,'vocab_3'=2,'seq'=4] {'vocab_1'}, dimensions={0}, use_global_device_ids=true | all-gather | bytes 9216 | tf_op jit(solution)/shard_map/all_gather | solution.py:55
  145.9 6.5 %all-gather.6 = f32[4,2,128]{2,1,0:T(2,128)S(1)} all-gather(f32[1,2,128]{2,1,0:T(2,128)S(1)} %maximum_bitcast_fusion.2), channel_id=4, replica_groups=mesh['vocab_0'=2,'vocab_1'=8,'vocab_2'=4,'vocab_3'=2,'seq'=4] {'vocab_2'}, dimensions={0}, use_global_device_ids=true | all-gather | bytes 5120 | tf_op jit(solution)/shard_map/all_gather | solution.py:55
  152.4 9.5 %all-gather.7 = f32[2,2,128]{2,1,0:T(2,128)S(1)} all-gather(f32[1,2,128]{2,1,0:T(2,128)S(1)} %maximum_bitcast_fusion.3), channel_id=5, replica_groups=mesh['vocab_0'=2,'vocab_1'=8,'vocab_2'=4,'vocab_3'=2,'seq'=4] {'vocab_3'}, dimensions={0}, use_global_device_ids=true | all-gather | bytes 3072 | tf_op jit(solution)/shard_map/all_gather | solution.py:55
  162.1 63.7 %while.13 = (s32[]{:T(128)}, f32[128]{0:T(128)S(1)}, f32[128]{0:T(128)S(1)}, f32[128,1024]{1,0:T(8,128)S(1)}, f32[128]{0:T(128)S(1)}, /*index=5*/f32[128,1024]{1...) while((s32[]{:T(128)}, f32[128]{0:T(128)S(1)}, f32[128]{0:T(128)S(1)}, ...), condition=%wide.region_8.9_spmd.clone, body=%wide.region_3.8_spmd.clone.sunk | while | flops 2778378 | bytes 1502415 | solution.py:142
  162.7 7.4 %all_to_all.43 = f32[8,128,7]{1,2,0:T(8,128)S(1)} all-to-all(f32[8,128,7]{1,2,0:T(8,128)S(1)} %broadcast_in_dim.72), channel_id=1, replica_groups=mesh['vocab_0'=2,'vocab_1'=8,'vocab_2'=4,'vocab_3'=2,'seq'=4] {'vocab_2'..., dimensions={0} | all-to-all | bytes 57344 | tf_op jit(solution)/shard_map/while/body/eval_jaxpr/all_to_all | solution.py:17
  170.8 5.0 %all-to-all-start.1 = ((f32[16,128,7]{1,2,0:T(8,128)}), f32[16,128,7]{1,2,0:T(8,128)S(1)}, u32[]{:S(2)}, u32[]{:S(2)}) async-start(f32[16,128,7]{1,2,0:T(8,128)} %broadcast_in_dim.73), calls=%async_computation.1 | async-start | bytes 131072 | tf_op jit(solution)/shard_map/while/body/eval_jaxpr/all_to_all | solution.py:17
  175.9 7.4 %all-to-all-done.1 = f32[16,128,7]{1,2,0:T(8,128)S(1)} async-done(((f32[16,128,7]{1,2,0:T(8,128)}), f32[16,128,7]{1,2,0:T(8,128)S(1)}, u32[]{:S(2)}, u32[]{:S(2)}) %all-to-all-start.1) | async-done | bytes 57376 | tf_op jit(solution)/shard_map/while/body/eval_jaxpr/all_to_all | solution.py:17
  183.9 9.2 %all_to_all.43 = f32[8,128,7]{1,2,0:T(8,128)S(1)} all-to-all(f32[8,128,7]{1,2,0:T(8,128)S(1)} %broadcast_in_dim.72), channel_id=1, replica_groups=mesh['vocab_0'=2,'vocab_1'=8,'vocab_2'=4,'vocab_3'=2,'seq'=4] {'vocab_2'..., dimensions={0} | all-to-all | bytes 57344 | tf_op jit(solution)/shard_map/while/body/eval_jaxpr/all_to_all | solution.py:17
  193.8 3.5 %all-to-all-start.1 = ((f32[16,128,7]{1,2,0:T(8,128)}), f32[16,128,7]{1,2,0:T(8,128)S(1)}, u32[]{:S(2)}, u32[]{:S(2)}) async-start(f32[16,128,7]{1,2,0:T(8,128)} %broadcast_in_dim.73), calls=%async_computation.1 | async-start | bytes 131072 | tf_op jit(solution)/shard_map/while/body/eval_jaxpr/all_to_all | solution.py:17
  197.3 7.3 %all-to-all-done.1 = f32[16,128,7]{1,2,0:T(8,128)S(1)} async-done(((f32[16,128,7]{1,2,0:T(8,128)}), f32[16,128,7]{1,2,0:T(8,128)S(1)}, u32[]{:S(2)}, u32[]{:S(2)}) %all-to-all-start.1) | async-done | bytes 57376 | tf_op jit(solution)/shard_map/while/body/eval_jaxpr/all_to_all | solution.py:17
  205.3 9.0 %all_to_all.43 = f32[8,128,7]{1,2,0:T(8,128)S(1)} all-to-all(f32[8,128,7]{1,2,0:T(8,128)S(1)} %broadcast_in_dim.72), channel_id=1, replica_groups=mesh['vocab_0'=2,'vocab_1'=8,'vocab_2'=4,'vocab_3'=2,'seq'=4] {'vocab_2'..., dimensions={0} | all-to-all | bytes 57344 | tf_op jit(solution)/shard_map/while/body/eval_jaxpr/all_to_all | solution.py:17
  214.9 3.5 %all-to-all-start.1 = ((f32[16,128,7]{1,2,0:T(8,128)}), f32[16,128,7]{1,2,0:T(8,128)S(1)}, u32[]{:S(2)}, u32[]{:S(2)}) async-start(f32[16,128,7]{1,2,0:T(8,128)} %broadcast_in_dim.73), calls=%async_computation.1 | async-start | bytes 131072 | tf_op jit(solution)/shard_map/while/body/eval_jaxpr/all_to_all | solution.py:17
  218.4 7.3 %all-to-all-done.1 = f32[16,128,7]{1,2,0:T(8,128)S(1)} async-done(((f32[16,128,7]{1,2,0:T(8,128)}), f32[16,128,7]{1,2,0:T(8,128)S(1)}, u32[]{:S(2)}, u32[]{:S(2)}) %all-to-all-start.1) | async-done | bytes 57376 | tf_op jit(solution)/shard_map/while/body/eval_jaxpr/all_to_all | solution.py:17
  (63 shorter events, 13.5 us)
Async XLA Ops:
  0.6 18.6 %copy-start = (s32[1,131072]{1,0:T(1,128)S(1)}, s32[1,131072]{1,0:T(1,128)}, u32[]{:S(2)}) copy-start(s32[1,131072]{1,0:T(1,128)} %param.13) | copy-start | bytes 1572868
  0.6 18.6 %copy-start.1 = (bf16[1,131072]{1,0:T(2,128)(2,1)S(1)}, bf16[1,131072]{1,0:T(2,128)(2,1)}, u32[]{:S(2)}) copy-start(bf16[1,131072]{1,0:T(2,128)(2,1)} %param.14) | copy-start | bytes 786436
  3.9 36.4 %all-to-all-start.3 = ((bf16[64,4,1792]{2,1,0:T(4,128)(2,1)}), bf16[64,4,1792]{2,1,0:T(4,128)(2,1)S(1)}, u32[]{:S(2)}, u32[]{:S(2)}) async-start(bf16[64,4,1792]{2,1,0:T(4,128)(2,1)} %broadcast_in_dim.20), calls=%async_computation.3 | async-start | bytes 1835008 | tf_op jit(solution)/shard_map/all_to_all | solution.py:17
  51.8 21.9 %all-to-all-start.2 = ((bf16[128,2,512]{2,1,0:T(2,128)(2,1)}), bf16[128,2,512]{2,1,0:T(2,128)(2,1)S(1)}, u32[]{:S(2)}, u32[]{:S(2)}) async-start(bf16[128,2,512]{2,1,0:T(2,128)(2,1)} %reshape.815), calls=%async_computation.2 | async-start | bytes 524288 | tf_op jit(solution)/shard_map/all_to_all | solution.py:101
  73.7 38.9 %all-to-all-start.5 = ((f32[4,128,1024]{2,1,0:T(8,128)}), f32[4,128,1024]{2,1,0:T(8,128)S(1)}, u32[]{:S(2)}, u32[]{:S(2)}) async-start(f32[4,128,1024]{2,1,0:T(8,128)} %fusion.4), calls=%async_computation.5 | async-start | bytes 4194304 | tf_op jit(solution)/shard_map/all_to_all | solution.py:43
  79.7 34.0 %copy-start.2 = (f32[128]{0:T(128)S(1)}, f32[128]{0:T(128)}, u32[]{:S(2)}) copy-start(f32[128]{0:T(128)} %param.18) | copy-start | bytes 1540
  79.7 34.0 %copy-start.3 = (f32[128]{0:T(128)S(1)}, f32[128]{0:T(128)}, u32[]{:S(2)}) copy-start(f32[128]{0:T(128)} %param.17) | copy-start | bytes 1540
  113.7 48.3 %copy-start.4 = (f32[128]{0:T(128)S(1)}, f32[128]{0:T(128)}, u32[]{:S(2)}) copy-start(f32[128]{0:T(128)} %param.19) | copy-start | bytes 1540
  170.8 12.4 %all-to-all-start.1 = ((f32[16,128,7]{1,2,0:T(8,128)}), f32[16,128,7]{1,2,0:T(8,128)S(1)}, u32[]{:S(2)}, u32[]{:S(2)}) async-start(f32[16,128,7]{1,2,0:T(8,128)} %broadcast_in_dim.73), calls=%async_computation.1 | async-start | bytes 131072 | tf_op jit(solution)/shard_map/while/body/eval_jaxpr/all_to_all | solution.py:17
  193.8 10.8 %all-to-all-start.1 = ((f32[16,128,7]{1,2,0:T(8,128)}), f32[16,128,7]{1,2,0:T(8,128)S(1)}, u32[]{:S(2)}, u32[]{:S(2)}) async-start(f32[16,128,7]{1,2,0:T(8,128)} %broadcast_in_dim.73), calls=%async_computation.1 | async-start | bytes 131072 | tf_op jit(solution)/shard_map/while/body/eval_jaxpr/all_to_all | solution.py:17
  214.9 10.8 %all-to-all-start.1 = ((f32[16,128,7]{1,2,0:T(8,128)}), f32[16,128,7]{1,2,0:T(8,128)S(1)}, u32[]{:S(2)}, u32[]{:S(2)}) async-start(f32[16,128,7]{1,2,0:T(8,128)} %broadcast_in_dim.73), calls=%async_computation.1 | async-start | bytes 131072 | tf_op jit(solution)/shard_map/while/body/eval_jaxpr/all_to_all | solution.py:17
where the time goes:
time: 227 us; the launch traced here: 226 us
  blocking collectives  80.4 us (35%)
  waiting for transfers between devices  78.2 us (34%)
  starting transfers between devices  41.7 us (18%)
  other arithmetic  9.74 us (4%)
  local copies, waits for them, and re-layouts  8.01 us (4%)
  matrix products  6.01 us (3%)
    all_gather x4, blocking collectives, gathered_once(): both, at, found = (lax.all_gather(jnp.concatenate(lines), axis), 0, {})  45.9 us
    all_to_all x4, waiting for transfers between devices, sent_to_all(): lax.all_to_all(jnp.broadcast_to(array[None], (count, *array.shape)), axis...  38.5 us
    all_to_all x4, blocking collectives, sent_to_all(): lax.all_to_all(jnp.broadcast_to(array[None], (count, *array.shape)), axis...  34.5 us
    all_to_all x1, waiting for transfers between devices, sum_at_owner(): lax.all_to_all(tiles, axis, split_axis=0, concat_axis=0, tiled=True)  32.2 us
    all_to_all x4, starting transfers between devices, sent_to_all(): lax.all_to_all(jnp.broadcast_to(array[None], (count, *array.shape)), axis...  27.4 us
    all_to_all x1, starting transfers between devices, per_device(): lax.all_to_all(offset, VOCAB, split_axis=1, concat_axis=0, tiled=True)  8.4 us
    all_to_all x1, waiting for transfers between devices, per_device(): lax.all_to_all(offset, VOCAB, split_axis=1, concat_axis=0, tiled=True)  7.52 us
    dot_general x1, matrix products, per_device(): jnp.dot(gather_axes(latent_vector, (('vocab_0', 'vocab_1', 'vocab_2'), 'v...  6.01 us
  transfers between devices with their start and end apart: 6, of which 6 were waited for; matrix products, arithmetic and copies ran while one was open for 5% of the time, Pallas kernels for 0%

commit v1 on v0

v1 whole, which is shorter than its diff:
```python
import functools

import jax
import jax.numpy as jnp
from jax import lax
from jax.experimental import pallas as pl
from jax.experimental.pallas import tpu as pltpu
from jax.sharding import Mesh
from jax.sharding import PartitionSpec as P

VOCAB = ("vocab_0", "vocab_1", "vocab_2", "vocab_3")
SEQ_VOCAB = ("seq", "vocab_0", "vocab_1", "vocab_2", "vocab_3")
MESH = pl.DeviceIdType.MESH
NEAR = 16
FAR = 8
LEVELS = (31, 15)
SPAN = 32.0


def sent_to_all(array, axis):
    count = lax.axis_size(axis)
    return lax.all_to_all(
        jnp.broadcast_to(array[None], (count, *array.shape)), axis, 0, 0, tiled=True
    )


def gather_axes(array, axes, dim):
    far, near = axes
    first = sent_to_all(array, far)
    tiles = jnp.swapaxes(sent_to_all(first, near), 0, 1)
    tiles = tiles.reshape(-1, *array.shape)
    return tiles.reshape(-1, array.shape[1])


def sum_at_owner(array, axis):
    count = lax.axis_size(axis)
    tiles = array.reshape(count, array.shape[0] // count, array.shape[1])
    arrived = lax.all_to_all(tiles, axis, split_axis=0, concat_axis=0, tiled=True)
    return arrived.sum(axis=0)


def near_index():
    return (
        lax.axis_index("vocab_0") * 8
        + lax.axis_index("vocab_2") * 2
        + lax.axis_index("vocab_3")
    )


def near_peer(index):
    return {
        "vocab_0": index // 8,
        "vocab_2": lax.rem(index // 2, 4),
        "vocab_3": lax.rem(index, 2),
    }


def far_peer(index):
    return {"vocab_1": index}


def exchange(held, me, count, peer, send_sem, recv_sem):
    copies = []
    for step in range(1, count):
        there = lax.rem(me + step, count)
        copy = pltpu.make_async_remote_copy(
            src_ref=held.at[me],
            dst_ref=held.at[me],
            send_sem=send_sem.at[step],
            recv_sem=recv_sem.at[step],
            device_id=peer(there),
            device_id_type=MESH,
        )
        copy.start()
        copies.append(copy)
    for step in range(1, count):
        source = lax.rem(me + count - step, count)
        pltpu.make_async_remote_copy(
            src_ref=held.at[me],
            dst_ref=held.at[source],
            send_sem=send_sem.at[step],
            recv_sem=recv_sem.at[step],
            device_id=peer(source),
            device_id_type=MESH,
        ).wait_recv()
    return copies


def reduced(values, near, far, sems, combine):
    here, there = near_index(), lax.axis_index("vocab_1")
    near[here] = values
    sent = exchange(near, here, NEAR, near_peer, sems[0], sems[1])
    part = near[0]
    for k in range(1, NEAR):
        part = combine(part, near[k])
    far[there] = part
    sent += exchange(far, there, FAR, far_peer, sems[2], sems[3])
    whole = far[0]
    for k in range(1, FAR):
        whole = combine(whole, far[k])
    return whole, sent


def masses(scores, weights, limits):
    rows = []
    chunks = scores.shape[0] // 8
    for start in range(0, len(limits), 8):
        group = [jnp.broadcast_to(t, (8, 128)) for t in limits[start : start + 8]]

        def add(k, sums, group=group):
            at = pl.ds(pl.multiple_of(k * 8, 8), 8)
            s, w = scores[at, :], weights[at, :]
            return tuple(a + jnp.where(s >= t, w, 0.0) for a, t in zip(sums, group))

        zero = jnp.zeros((8, 128), jnp.float32)
        sums = lax.fori_loop(0, chunks, add, (zero,) * len(group), unroll=8)
        rows += [jnp.sum(a, axis=0, keepdims=True) for a in sums]
    return rows


def tail_kernel(
    logits,
    offset,
    divisor,
    softening,
    share,
    out,
    cutoff,
    scores,
    weights,
    near_a,
    far_a,
    near_b,
    far_b,
    near_c,
    far_c,
    sem_near_send,
    sem_near_recv,
    sem_far_send,
    sem_far_recv,
):
    barrier = pltpu.get_barrier_semaphore()
    here, there = near_index(), lax.axis_index("vocab_1")
    for step in range(1, NEAR):
        pl.semaphore_signal(
            barrier, inc=1, device_id=near_peer(lax.rem(here + step, NEAR)), device_id_type=MESH
        )
    for step in range(1, FAR):
        pl.semaphore_signal(
            barrier, inc=1, device_id=far_peer(lax.rem(there + step, FAR)), device_id_type=MESH
        )

    inverse = 1.0 / divisor[...]
    cooler = 1.0 / softening[...]
    highest = None
    for k in range(logits.shape[1] // 128):
        at = pl.ds(k * 128, 128)
        raw, shift = logits[:, at], offset[:, at].astype(jnp.float32)
        scaled = jnp.where(raw > 0, raw * inverse, raw * divisor[...])
        changed = jnp.where(shift < 0, scaled, raw) + shift
        out[:, at] = changed.astype(jnp.bfloat16)
        turned = (changed * cooler).T
        scores[at, :] = turned
        most = jnp.max(turned, axis=0, keepdims=True)
        highest = most if highest is None else jnp.maximum(highest, most)
    pl.semaphore_wait(barrier, NEAR + FAR - 2)

    def sems(turn):
        return (
            sem_near_send.at[turn],
            sem_near_recv.at[turn],
            sem_far_send.at[turn],
            sem_far_recv.at[turn],
        )

    largest, sent = reduced(highest, near_a, far_a, sems(0), jnp.maximum)
    total = jnp.zeros((8, 128), jnp.float32)
    chunk = 64
    for k in range(scores.shape[0] // chunk):
        at = pl.ds(k * chunk, chunk)
        terms = jnp.exp(scores[at, :] - largest)
        weights[at, :] = terms
        total = total + jnp.sum(terms.reshape(chunk // 8, 8, 128), axis=0)

    first = [largest - (SPAN / (LEVELS[0] + 1)) * (k + 1) for k in range(LEVELS[0])]
    rows = [jnp.sum(total, axis=0, keepdims=True)] + masses(scores, weights, first)
    sums, more = reduced(jnp.concatenate(rows), near_b, far_b, sems(1), jnp.add)
    sent += more
    target = share[...] * sums[0:1]
    lower = jnp.sum(
        jnp.where(sums[1:] < target, 1.0, 0.0), axis=0, keepdims=True
    ) * (LEVELS[1] + 1)

    unit = SPAN / ((LEVELS[0] + 1) * (LEVELS[1] + 1))
    second = [largest - unit * (lower + (k + 1)) for k in range(LEVELS[1])]
    rows = masses(scores, weights, second)
    rows.append(rows[-1])
    sums, more = reduced(jnp.concatenate(rows), near_c, far_c, sems(2), jnp.add)
    sent += more
    below = jnp.where(sums[: LEVELS[1]] < target, 1.0, 0.0)
    lower = lower + jnp.sum(below, axis=0, keepdims=True)
    cutoff[...] = largest - unit * (lower + 1.0)
    for copy in sent:
        copy.wait_send()


def tail(logits, offset, divisor, softening, share):
    rows, columns = logits.shape
    vmem = pl.BlockSpec(memory_space=pltpu.VMEM)

    def held(count, depth):
        return pltpu.VMEM((count, depth, 128), jnp.float32)

    return pl.pallas_call(
        tail_kernel,
        out_shape=(
            jax.ShapeDtypeStruct((rows, columns), jnp.bfloat16),
            jax.ShapeDtypeStruct((1, rows), jnp.float32),
        ),
        in_specs=[vmem] * 5,
        out_specs=(vmem, vmem),
        scratch_shapes=[
            pltpu.VMEM((columns, rows), jnp.float32),
            pltpu.VMEM((columns, rows), jnp.float32),
            held(NEAR, 1),
            held(FAR, 1),
            held(NEAR, LEVELS[0] + 1),
            held(FAR, LEVELS[0] + 1),
            held(NEAR, LEVELS[1] + 1),
            held(FAR, LEVELS[1] + 1),
            pltpu.SemaphoreType.DMA((3, NEAR)),
            pltpu.SemaphoreType.DMA((3, NEAR)),
            pltpu.SemaphoreType.DMA((3, FAR)),
            pltpu.SemaphoreType.DMA((3, FAR)),
        ],
        compiler_params=pltpu.CompilerParams(collective_id=1, has_side_effects=True),
        name="tail",
    )(logits, offset, divisor[:, None], softening[:, None], share[None, :])


def per_device(
    latent_vector,
    unembedding_matrix,
    occurrence_tally,
    additive_offset_table,
    recurrence_charge,
    appearance_charge,
    recurrence_divisor,
    softening_divisor,
    nucleus_share_limit,
):
    count_float = occurrence_tally.astype(jnp.float32)
    offset = (
        additive_offset_table.astype(jnp.float32)
        - recurrence_charge[:, None] * count_float
        - appearance_charge[:, None] * (occurrence_tally > 0).astype(jnp.float32)
    ).astype(jnp.bfloat16)
    relaid = lax.all_to_all(offset, VOCAB, split_axis=1, concat_axis=0, tiled=True)
    partial_logits = jnp.dot(
        gather_axes(latent_vector, (("vocab_0", "vocab_1", "vocab_2"), "vocab_3"), 0),
        unembedding_matrix,
        preferred_element_type=jnp.float32,
    )
    logits = sum_at_owner(partial_logits, "seq")
    out, cutoff = tail(
        logits, relaid, recurrence_divisor, softening_divisor, nucleus_share_limit
    )
    return out, cutoff.reshape(-1)


def solution(mesh):
    split = Mesh(
        mesh.devices.reshape(2, 8, 4, 2, mesh.shape["seq"]),
        ("vocab_0", "vocab_1", "vocab_2", "vocab_3", "seq"),
    )
    placed = (
        P(VOCAB, "seq"),
        P("seq", VOCAB),
        P(SEQ_VOCAB, None),
        P(SEQ_VOCAB, None),
        P(SEQ_VOCAB),
        P(SEQ_VOCAB),
        P("seq"),
        P("seq"),
        P("seq"),
    )
    return jax.shard_map(
        per_device,
        mesh=split,
        in_specs=placed,
        out_specs=(P("seq", VOCAB), P("seq")),
        check_vma=False,
    )
```

time: 227 us -> 168 us (0.74)
  blocking collectives: 80.4 us -> 8.87 us
  Pallas kernels: 0 us -> 54.8 us
  waiting for transfers between devices: 78.2 us -> 48.9 us
  starting transfers between devices: 41.7 us -> 29.7 us
  local copies, waits for them, and re-layouts: 8.01 us -> 13.9 us
  other arithmetic: 9.74 us -> 4.21 us
    pallas_call x0 -> x1, Pallas kernels: none -> 54.8 us  [tail(): pl.pallas_call(tail_kernel, out_shape=(jax.ShapeDtypeStruct((rows, column...]
    all_gather x4 -> x0, blocking collectives: 45.9 us -> none  [gathered_once(): both, at, found = (lax.all_gather(jnp.concatenate(lines), axis), 0, {})]
    all_to_all x4 -> x1, blocking collectives: 34.5 us -> 8.87 us  [sent_to_all(): lax.all_to_all(jnp.broadcast_to(array[None], (count, *array.shape)), axis...]
    all_to_all x4 -> x1, waiting for transfers between devices: 38.5 us -> 15.1 us  [sent_to_all(): lax.all_to_all(jnp.broadcast_to(array[None], (count, *array.shape)), axis...]
    all_to_all x4 -> x1, starting transfers between devices: 27.4 us -> 15.3 us  [sent_to_all(): lax.all_to_all(jnp.broadcast_to(array[None], (count, *array.shape)), axis...]
    all_to_all x1, waiting for transfers between devices: 7.52 us -> 3.26 us  [per_device(): lax.all_to_all(offset, VOCAB, split_axis=1, concat_axis=0, tiled=True)]
    unnamed x13 -> x14, local copies, waits for them, and re-layouts: 1.65 us -> 5.19 us
  transfers between devices with their start and end apart: 6 -> 3, of which waited for: 6 -> 3; matrix products, arithmetic and copies ran while one was open for 5% -> 10% of each run, Pallas kernels for 0% -> 0%
where the time goes in v1:
time: 168 us
  Pallas kernels  54.8 us (33%)
  waiting for transfers between devices  48.9 us (29%)
  starting transfers between devices  29.7 us (18%)
  local copies, waits for them, and re-layouts  13.9 us (8%)
  blocking collectives  8.87 us (5%)
  matrix products  5.44 us (3%)
  other arithmetic  4.21 us (3%)
  between operations  2.02 us (1%)
    pallas_call x1, Pallas kernels, tail(): pl.pallas_call(tail_kernel, out_shape=(jax.ShapeDtypeStruct((rows, column...  54.8 us
    all_to_all x1, waiting for transfers between devices, sum_at_owner(): lax.all_to_all(tiles, axis, split_axis=0, concat_axis=0, tiled=True)  30.5 us
    all_to_all x1, starting transfers between devices, sent_to_all(): lax.all_to_all(jnp.broadcast_to(array[None], (count, *array.shape)), axis...  15.3 us
    all_to_all x1, waiting for transfers between devices, sent_to_all(): lax.all_to_all(jnp.broadcast_to(array[None], (count, *array.shape)), axis...  15.1 us
    all_to_all x1, blocking collectives, sent_to_all(): lax.all_to_all(jnp.broadcast_to(array[None], (count, *array.shape)), axis...  8.87 us
    all_to_all x1, starting transfers between devices, per_device(): lax.all_to_all(offset, VOCAB, split_axis=1, concat_axis=0, tiled=True)  8.4 us
    all_to_all x1, starting transfers between devices, sum_at_owner(): lax.all_to_all(tiles, axis, split_axis=0, concat_axis=0, tiled=True)  5.92 us
    dot_general x1, matrix products, per_device(): jnp.dot(gather_axes(latent_vector, (('vocab_0', 'vocab_1', 'vocab_2'), 'v...  5.44 us
  transfers between devices with their start and end apart: 3, of which 3 were waited for; matrix products, arithmetic and copies ran while one was open for 10% of the time, Pallas kernels for 0%

profile of v1, /device:TPU:1, one launch (start us, length us, event | category | flops | bytes accessed | tf_op | source)
XLA Modules:
  0.0 167.8 jit_solution(14051444129032320283)
XLA Ops:
  0.6 2.0 %broadcast_in_dim.10 = bf16[64,4,1792]{2,1,0:T(4,128)(2,1)} broadcast(bf16[4,1792]{1,0:T(4,128)(2,1)} %param.9), dimensions={1,2} | broadcast | bytes 931840 | tf_op jit(solution)/shard_map/broadcast_in_dim | solution.py:23
  2.6 15.3 %all-to-all-start = ((bf16[64,4,1792]{2,1,0:T(4,128)(2,1)}), bf16[64,4,1792]{2,1,0:T(4,128)(2,1)S(1)}, u32[]{:S(2)}, u32[]{:S(2)}) async-start(bf16[64,4,1792]{2,1,0:T(4,128)(2,1)} %broadcast_in_dim.10), calls=%async_computation | async-start | bytes 1835008 | tf_op jit(solution)/shard_map/all_to_all | solution.py:22
  19.3 1.1 fusion.3
  20.4 0.5 broadcast.9
  20.9 2.1 %reduce = bf16[128,1024]{1,0:T(8,128)(2,1)S(1)} reduce(bf16[128,1,1024]{2,1,0:T(2,128)(2,1)S(1)} %bitcast.21, bf16[]{:T(256)} %broadcast.9), dimensions={1}, to_apply=%bitcast.13.reduce_sub_computation | reduce | bytes 524290
  23.0 0.9 reshape.26
  23.9 15.1 %all-to-all-done = bf16[64,4,1792]{2,1,0:T(4,128)(2,1)S(1)} async-done(((bf16[64,4,1792]{2,1,0:T(4,128)(2,1)}), bf16[64,4,1792]{2,1,0:T(4,128)(2,1)S(1)}, u32[]{:S(2)}, u32[]{:S(2)}) %all-to-all-start) | async-done | bytes 917536 | tf_op jit(solution)/shard_map/all_to_all | solution.py:22
  39.1 0.5 broadcast_in_dim.11
  39.5 8.9 %all_to_all.31 = bf16[2,64,4,1792]{3,2,1,0:T(4,128)(2,1)S(1)} all-to-all(bf16[2,64,4,1792]{3,2,1,0:T(4,128)(2,1)S(1)} %broadcast_in_dim.11), channel_id=1, replica_groups=mesh['vocab_0'=2,'vocab_1'=8,'vocab_2'=4,'vocab_3'=2,'seq'=4] {'vocab_3'}, dimensions={0} | all-to-all | bytes 3670016 | tf_op jit(solution)/shard_map/all_to_all | solution.py:22
  48.4 8.4 %all-to-all-start.3 = ((bf16[128,2,512]{2,1,0:T(2,128)(2,1)}), bf16[128,2,512]{2,1,0:T(2,128)(2,1)S(1)}, u32[]{:S(2)}, u32[]{:S(2)}) async-start(bf16[128,2,512]{2,1,0:T(2,128)(2,1)} %reshape.26), calls=%async_computation.3 | async-start | bytes 524288 | tf_op jit(solution)/shard_map/all_to_all | solution.py:258
  56.8 1.9 %copy.16 = bf16[64,2,4,1792]{3,2,1,0:T(4,128)(2,1)} copy(bf16[64,2,4,1792]{3,2,0,1:T(4,128)(2,1)S(1)} %bitcast.19) | data formatting | bytes 3670016 | tf_op jit(solution)/shard_map/transpose | solution.py:30
  58.7 2.9 %dot_general.5 = bf16[4,128,1792]{2,1,0:T(8,128)(2,1)S(1)} reshape(bf16[64,2,4,1792]{3,2,1,0:T(4,128)(2,1)} %copy.16) | data formatting | bytes 3670016 | tf_op jit(solution)/shard_map/dot_general | solution.py:259
  61.6 5.4 %fusion = f32[4,128,1024]{2,1,0:T(8,128)} fusion(bf16[4,128,1792]{2,1,0:T(8,128)(2,1)S(1)} %dot_general.5, bf16[1792,1024]{1,0:T(8,128)(2,1)} %param.10), kind=kOutput, calls=%fused_computation | convolution fusion | flops 1879048192 | bytes 7602176 | tf_op jit(solution)/shard_map/dot_general | solution.py:259
  67.1 3.3 %all-to-all-done.3 = bf16[128,2,512]{2,1,0:T(2,128)(2,1)S(1)} async-done(((bf16[128,2,512]{2,1,0:T(2,128)(2,1)}), bf16[128,2,512]{2,1,0:T(2,128)(2,1)S(1)}, u32[]{:S(2)}, u32[]{:S(2)}) %all-to-all-start.3) | async-done | bytes 262176 | tf_op jit(solution)/shard_map/all_to_all | solution.py:258
  70.3 5.9 %all-to-all-start.2 = ((f32[4,128,1024]{2,1,0:T(8,128)}), f32[4,128,1024]{2,1,0:T(8,128)S(1)}, u32[]{:S(2)}, u32[]{:S(2)}) async-start(f32[4,128,1024]{2,1,0:T(8,128)} %fusion), calls=%async_computation.2 | async-start | bytes 4194304 | tf_op jit(solution)/shard_map/all_to_all | solution.py:38
  76.3 0.7 copy.17.divisor
  77.0 0.7 copy.18.softening
  77.7 0.2 reshape.27
  78.0 0.8 copy.21
  78.7 30.5 %all-to-all-done.2 = f32[4,128,1024]{2,1,0:T(8,128)S(1)} async-done(((f32[4,128,1024]{2,1,0:T(8,128)}), f32[4,128,1024]{2,1,0:T(8,128)S(1)}, u32[]{:S(2)}, u32[]{:S(2)}) %all-to-all-start.2) | async-done | bytes 2097184 | tf_op jit(solution)/shard_map/all_to_all | solution.py:38
  109.3 1.0 reduce_sum.9.logits
  110.3 54.8 %tail.1 = (bf16[128,1024]{1,0:T(8,128)(2,1)}, f32[1,128]{1,0:T(1,128)}) custom-call(f32[128,1024]{1,0:T(8,128)} %reduce_sum.9.logits, bf16[128,1024]{1,0:T(8,128)(2,1)} %bitcast.22, f32[128,1]{1,0:T(8,128)} %copy.17.divisor, f32[128,1]{1,0:T(8,128)} %copy.18.softening, f32[1,128]{1,0:T(1,128)} %bitcast.25), custom_call_target="tpu_custom_call" | custom-call | tf_op jit(solution)/shard_map/tail/pallas_call | solution.py:214
  165.1 1.7 copy.26
  166.7 1.1 copy.27
  (8 shorter events, 0.0 us)
Async XLA Ops:
  0.6 18.6 %copy-start = (s32[1,131072]{1,0:T(1,128)S(1)}, s32[1,131072]{1,0:T(1,128)}, u32[]{:S(2)}) copy-start(s32[1,131072]{1,0:T(1,128)} %param.11) | copy-start | bytes 1572868
  0.6 18.6 %copy-start.1 = (bf16[1,131072]{1,0:T(2,128)(2,1)S(1)}, bf16[1,131072]{1,0:T(2,128)(2,1)}, u32[]{:S(2)}) copy-start(bf16[1,131072]{1,0:T(2,128)(2,1)} %param.12) | copy-start | bytes 786436
  2.6 36.4 %all-to-all-start = ((bf16[64,4,1792]{2,1,0:T(4,128)(2,1)}), bf16[64,4,1792]{2,1,0:T(4,128)(2,1)S(1)}, u32[]{:S(2)}, u32[]{:S(2)}) async-start(bf16[64,4,1792]{2,1,0:T(4,128)(2,1)} %broadcast_in_dim.10), calls=%async_computation | async-start | bytes 1835008 | tf_op jit(solution)/shard_map/all_to_all | solution.py:22
  48.4 21.9 %all-to-all-start.3 = ((bf16[128,2,512]{2,1,0:T(2,128)(2,1)}), bf16[128,2,512]{2,1,0:T(2,128)(2,1)S(1)}, u32[]{:S(2)}, u32[]{:S(2)}) async-start(bf16[128,2,512]{2,1,0:T(2,128)(2,1)} %reshape.26), calls=%async_computation.3 | async-start | bytes 524288 | tf_op jit(solution)/shard_map/all_to_all | solution.py:258
  67.1 9.2 %copy-start.2 = (f32[128]{0:T(128)S(1)}, f32[128]{0:T(128)}, u32[]{:S(2)}) copy-start(f32[128]{0:T(128)} %param.15) | copy-start | bytes 1540
  67.1 9.9 %copy-start.3 = (f32[128]{0:T(128)S(1)}, f32[128]{0:T(128)}, u32[]{:S(2)}) copy-start(f32[128]{0:T(128)} %param.16) | copy-start | bytes 1540
  70.3 38.9 %all-to-all-start.2 = ((f32[4,128,1024]{2,1,0:T(8,128)}), f32[4,128,1024]{2,1,0:T(8,128)S(1)}, u32[]{:S(2)}, u32[]{:S(2)}) async-start(f32[4,128,1024]{2,1,0:T(8,128)} %fusion), calls=%async_computation.2 | async-start | bytes 4194304 | tf_op jit(solution)/shard_map/all_to_all | solution.py:38

commit v2 on v1

--- a/solution.py
+++ b/solution.py
@@ -1,4 +1,4 @@
-import functools
+import itertools
 
 import jax
 import jax.numpy as jnp
@@ -15,28 +15,8 @@
 FAR = 8
 LEVELS = (31, 15)
 SPAN = 32.0
-
-
-def sent_to_all(array, axis):
-    count = lax.axis_size(axis)
-    return lax.all_to_all(
-        jnp.broadcast_to(array[None], (count, *array.shape)), axis, 0, 0, tiled=True
-    )
-
-
-def gather_axes(array, axes, dim):
-    far, near = axes
-    first = sent_to_all(array, far)
-    tiles = jnp.swapaxes(sent_to_all(first, near), 0, 1)
-    tiles = tiles.reshape(-1, *array.shape)
-    return tiles.reshape(-1, array.shape[1])
-
-
-def sum_at_owner(array, axis):
-    count = lax.axis_size(axis)
-    tiles = array.reshape(count, array.shape[0] // count, array.shape[1])
-    arrived = lax.all_to_all(tiles, axis, split_axis=0, concat_axis=0, tiled=True)
-    return arrived.sum(axis=0)
+PARTS = 4
+COPIES = 96
 
 
 def near_index():
@@ -118,52 +98,242 @@
     return rows
 
 
-def tail_kernel(
-    logits,
+def step_kernel(
+    latent,
+    weights_hbm,
     offset,
     divisor,
     softening,
     share,
     out,
     cutoff,
+    weights,
+    few,
+    hidden,
+    partial,
+    relay_in,
+    direct_in,
+    final_in,
+    far_offset,
+    near_offset,
     scores,
-    weights,
+    terms,
     near_a,
     far_a,
     near_b,
     far_b,
     near_c,
     far_c,
+    send_sem,
+    recv_sem,
+    local_sem,
     sem_near_send,
     sem_near_recv,
     sem_far_send,
     sem_far_recv,
 ):
+    y, z = lax.axis_index("vocab_0"), lax.axis_index("vocab_1")
+    x, core = lax.axis_index("vocab_2"), lax.axis_index("vocab_3")
+    seq = lax.axis_index("seq")
+    here, pair = near_index(), x * 2 + core
+    half = latent.shape[1] // 2
+    rows, columns = out.shape
+    mid, wide = rows // 2, columns // PARTS
+
+    load = pltpu.make_async_copy(weights_hbm, weights, local_sem.at[0])
+    load.start()
     barrier = pltpu.get_barrier_semaphore()
-    here, there = near_index(), lax.axis_index("vocab_1")
+
+    def greet(peer):
+        pl.semaphore_signal(barrier, inc=1, device_id=peer, device_id_type=MESH)
+
     for step in range(1, NEAR):
-        pl.semaphore_signal(
-            barrier, inc=1, device_id=near_peer(lax.rem(here + step, NEAR)), device_id_type=MESH
-        )
+        greet(near_peer(lax.rem(here + step, NEAR)))
     for step in range(1, FAR):
-        pl.semaphore_signal(
-            barrier, inc=1, device_id=far_peer(lax.rem(there + step, FAR)), device_id_type=MESH
-        )
+        greet(far_peer(lax.rem(z + step, FAR)))
+    after, before = {"seq": lax.rem(seq + 1, 4)}, {"seq": lax.rem(seq + 3, 4)}
+    greet(after)
+    greet(before)
+
+    numbers = itertools.count()
+    sent = []
+
+    def describe(number, source, target, peer):
+        return pltpu.make_async_remote_copy(
+            src_ref=source,
+            dst_ref=target,
+            send_sem=send_sem.at[number],
+            recv_sem=recv_sem.at[number],
+            device_id=peer,
+            device_id_type=MESH,
+        )
+
+    def send(source, target, peer):
+        number = next(numbers)
+        copy = describe(number, source, target, peer)
+        copy.start()
+        sent.append(copy)
+        return number
+
+    def arrive(number, landing, peer):
+        describe(number, landing, landing, peer).wait_recv()
+
+    def my_half(which):
+        return pl.ds(pl.multiple_of(which * half, 128), half)
+
+    few[pair] = latent[:, my_half(core)]
+    pl.semaphore_wait(barrier, NEAR + FAR)
+
+    def pair_peer(index):
+        return {"vocab_2": index // 2, "vocab_3": lax.rem(index, 2)}
+
+    order = [4, 5, 3, 1, 2, 6, 7]
+    swaps = {}
+    for step in order:
+        there = lax.rem(pair + step, 8)
+        swaps[step] = send(
+            latent.at[:, my_half(lax.rem(there, 2))], few.at[pair], pair_peer(there)
+        )
+    for step in order:
+        source = lax.rem(pair + 8 - step, 8)
+        arrive(swaps[step], few.at[source], pair_peer(source))
+    joined = jnp.concatenate([few[k].astype(jnp.float32) for k in range(8)])
+
+    def block(which_y, which_z):
+        at = pl.multiple_of((which_y * FAR + which_z) * 32, 32)
+        return hidden.at[core, pl.ds(at, 32)]
+
+    hidden[core, pl.ds(pl.multiple_of((y * FAR + z) * 32, 32), 32)] = joined.astype(
+        jnp.bfloat16
+    )
+
+    other_core, other_y = {"vocab_3": 1 - core}, {"vocab_0": 1 - y}
+    up, down = {"vocab_1": lax.rem(z + 1, FAR)}, {"vocab_1": lax.rem(z + 7, FAR)}
+    shares = []
+
+    def to_core(which_y, which_z):
+        number = send(block(which_y, which_z), block(which_y, which_z), other_core)
+        at = pl.multiple_of((which_y * FAR + which_z) * 32, 32)
+        shares.append((number, hidden.at[1 - core, pl.ds(at, 32)]))
+
+    def pass_on(which_y, which_z, way):
+        piece = block(which_y, which_z)
+        return send(piece, piece, up if way == 0 else down)
+
+    ring = {}
+    mine = [y, 1 - y]
+    across = send(block(y, z), block(y, z), other_y)
+    for way in range(2):
+        ring[way, 0, 0] = pass_on(y, z, way)
+    arrive(across, block(1 - y, z), other_y)
+    for way in range(2):
+        ring[way, 0, 1] = pass_on(1 - y, z, way)
+    to_core(y, z)
+    to_core(1 - y, z)
+    for step in range(1, 5):
+        for k in range(2):
+            for way in range(2):
+                if step == 4 and way != k:
+                    continue
+                came = lax.rem(z + (8 - step if way == 0 else step), FAR)
+                arrive(ring[way, step - 1, k], block(mine[k], came), down if way == 0 else up)
+                if step < 3 or (step == 3 and way == k):
+                    ring[way, step, k] = pass_on(mine[k], came, way)
+                to_core(mine[k], came)
+
+    far_copies = []
+    for step in range(1, FAR):
+        there = lax.rem(z + step, FAR)
+        far_copies.append(send(offset.at[:, there], far_offset.at[z], far_peer(there)))
+    own = pltpu.make_async_copy(offset.at[:, z], far_offset.at[z], local_sem.at[1])
+    own.start()
+
+    load.wait()
+    for number, landing in shares:
+        arrive(number, landing, other_core)
+
+    def multiply(slot, target):
+        at = pl.ds(pl.multiple_of(target * rows, rows), rows)
+        for k in range(PARTS):
+            cut = pl.ds(k * wide, wide)
+            partial[slot, :, cut] = jnp.dot(
+                hidden[0, at, :], weights[:half, cut], preferred_element_type=jnp.float32
+            ) + jnp.dot(
+                hidden[1, at, :], weights[half:, cut], preferred_element_type=jnp.float32
+            )
+            yield cut
+
+    first, last = pl.ds(0, mid), pl.ds(mid, mid)
+    relays = []
+    for k, cut in enumerate(multiply(0, lax.rem(seq + 2, 4))):
+        relays.append(
+            (
+                send(partial.at[0, first, cut], relay_in.at[0, :, cut], after),
+                send(partial.at[0, last, cut], relay_in.at[1, :, cut], before),
+            )
+        )
+    directs = []
+    for cut in multiply(1, lax.rem(seq + 1, 4)):
+        directs.append([send(partial.at[1, last, cut], direct_in.at[0, :, cut], after)])
+    for k, cut in enumerate(multiply(2, lax.rem(seq + 3, 4))):
+        directs[k].append(send(partial.at[2, first, cut], direct_in.at[1, :, cut], before))
+    finals = []
+    for k in range(PARTS):
+        cut = pl.ds(k * wide, wide)
+        arrive(relays[k][0], relay_in.at[0, :, cut], before)
+        partial[1, first, cut] += relay_in[0, :, cut]
+        one = send(partial.at[1, first, cut], final_in.at[0, :, cut], after)
+        arrive(relays[k][1], relay_in.at[1, :, cut], after)
+        partial[2, last, cut] += relay_in[1, :, cut]
+        finals.append((one, send(partial.at[2, last, cut], final_in.at[1, :, cut], before)))
+    for cut in multiply(3, seq):
+        pass
+
+    own.wait()
+    for step in range(1, FAR):
+        source = lax.rem(z + FAR - step, FAR)
+        arrive(far_copies[step - 1], far_offset.at[source], far_peer(source))
+
+    def landed(index):
+        return near_offset.at[index // 8, :, lax.rem(index, 8)]
+
+    near_copies = []
+    for step in range(1, NEAR):
+        there = lax.rem(here + step, NEAR)
+        near_copies.append(
+            send(
+                far_offset.at[:, there // 8, lax.rem(there, 8)], landed(here), near_peer(there)
+            )
+        )
+    own = pltpu.make_async_copy(far_offset.at[:, y, pair], landed(here), local_sem.at[2])
+    own.start()
+    own.wait()
+    for step in range(1, NEAR):
+        source = lax.rem(here + NEAR - step, NEAR)
+        arrive(near_copies[step - 1], landed(source), near_peer(source))
 
     inverse = 1.0 / divisor[...]
     cooler = 1.0 / softening[...]
     highest = None
-    for k in range(logits.shape[1] // 128):
-        at = pl.ds(k * 128, 128)
-        raw, shift = logits[:, at], offset[:, at].astype(jnp.float32)
-        scaled = jnp.where(raw > 0, raw * inverse, raw * divisor[...])
-        changed = jnp.where(shift < 0, scaled, raw) + shift
-        out[:, at] = changed.astype(jnp.bfloat16)
-        turned = (changed * cooler).T
-        scores[at, :] = turned
-        most = jnp.max(turned, axis=0, keepdims=True)
-        highest = most if highest is None else jnp.maximum(highest, most)
-    pl.semaphore_wait(barrier, NEAR + FAR - 2)
+    for k in range(PARTS):
+        cut = pl.ds(k * wide, wide)
+        arrive(directs[k][0], direct_in.at[0, :, cut], before)
+        arrive(directs[k][1], direct_in.at[1, :, cut], after)
+        arrive(finals[k][0], final_in.at[0, :, cut], before)
+        arrive(finals[k][1], final_in.at[1, :, cut], after)
+        for j in range(k * wide // 128, (k + 1) * wide // 128):
+            at = pl.ds(j * 128, 128)
+            upper = partial[3, first, at] + (final_in[0, :, at] + direct_in[1, :, at])
+            lower = partial[3, last, at] + (final_in[1, :, at] + direct_in[0, :, at])
+            raw = jnp.concatenate([upper, lower])
+            shift = near_offset[:, :, :, j, :].reshape(rows, 128)
+            scaled = jnp.where(raw > 0, raw * inverse, raw * divisor[...])
+            changed = jnp.where(shift < 0, scaled, raw) + shift
+            out[:, at] = changed.astype(jnp.bfloat16)
+            turned = (changed * cooler).T
+            scores[at, :] = turned
+            most = jnp.max(turned, axis=0, keepdims=True)
+            highest = most if highest is None else jnp.maximum(highest, most)
 
     def sems(turn):
         return (
@@ -173,17 +343,18 @@
             sem_far_recv.at[turn],
         )
 
-    largest, sent = reduced(highest, near_a, far_a, sems(0), jnp.maximum)
+    largest, more = reduced(highest, near_a, far_a, sems(0), jnp.maximum)
+    sent += more
     total = jnp.zeros((8, 128), jnp.float32)
     chunk = 64
     for k in range(scores.shape[0] // chunk):
         at = pl.ds(k * chunk, chunk)
-        terms = jnp.exp(scores[at, :] - largest)
-        weights[at, :] = terms
-        total = total + jnp.sum(terms.reshape(chunk // 8, 8, 128), axis=0)
+        grown = jnp.exp(scores[at, :] - largest)
+        terms[at, :] = grown
+        total = total + jnp.sum(grown.reshape(chunk // 8, 8, 128), axis=0)
 
     first = [largest - (SPAN / (LEVELS[0] + 1)) * (k + 1) for k in range(LEVELS[0])]
-    rows = [jnp.sum(total, axis=0, keepdims=True)] + masses(scores, weights, first)
+    rows = [jnp.sum(total, axis=0, keepdims=True)] + masses(scores, terms, first)
     sums, more = reduced(jnp.concatenate(rows), near_b, far_b, sems(1), jnp.add)
     sent += more
     target = share[...] * sums[0:1]
@@ -193,7 +364,7 @@
 
     unit = SPAN / ((LEVELS[0] + 1) * (LEVELS[1] + 1))
     second = [largest - unit * (lower + (k + 1)) for k in range(LEVELS[1])]
-    rows = masses(scores, weights, second)
+    rows = masses(scores, terms, second)
     rows.append(rows[-1])
     sums, more = reduced(jnp.concatenate(rows), near_c, far_c, sems(2), jnp.add)
     sent += more
@@ -204,38 +375,56 @@
         copy.wait_send()
 
 
-def tail(logits, offset, divisor, softening, share):
-    rows, columns = logits.shape
+def step(latent, weights, offset, divisor, softening, share, rows):
+    columns = weights.shape[1]
     vmem = pl.BlockSpec(memory_space=pltpu.VMEM)
-
-    def held(count, depth):
-        return pltpu.VMEM((count, depth, 128), jnp.float32)
+    depth = weights.shape[0]
+
+    def held(count, lines):
+        return pltpu.VMEM((count, lines, 128), jnp.float32)
+
+    def whole(*shape):
+        return pltpu.VMEM(shape, jnp.float32)
 
     return pl.pallas_call(
-        tail_kernel,
+        step_kernel,
         out_shape=(
             jax.ShapeDtypeStruct((rows, columns), jnp.bfloat16),
             jax.ShapeDtypeStruct((1, rows), jnp.float32),
         ),
-        in_specs=[vmem] * 5,
+        in_specs=[vmem, pl.BlockSpec(memory_space=pl.ANY)] + [vmem] * 4,
         out_specs=(vmem, vmem),
         scratch_shapes=[
-            pltpu.VMEM((columns, rows), jnp.float32),
-            pltpu.VMEM((columns, rows), jnp.float32),
+            pltpu.VMEM((depth, columns), weights.dtype),
+            pltpu.VMEM((8, latent.shape[0], depth // 2), latent.dtype),
+            pltpu.VMEM((2, 4 * rows, depth // 2), latent.dtype),
+            whole(4, rows, columns),
+            whole(2, rows // 2, columns),
+            whole(2, rows // 2, columns),
+            whole(2, rows // 2, columns),
+            whole(FAR, 2, 8, columns // 128, 128),
+            whole(2, FAR, 8, columns // 128, 128),
+            whole(columns, rows),
+            whole(columns, rows),
             held(NEAR, 1),
             held(FAR, 1),
             held(NEAR, LEVELS[0] + 1),
             held(FAR, LEVELS[0] + 1),
             held(NEAR, LEVELS[1] + 1),
             held(FAR, LEVELS[1] + 1),
+            pltpu.SemaphoreType.DMA((COPIES,)),
+            pltpu.SemaphoreType.DMA((COPIES,)),
+            pltpu.SemaphoreType.DMA((3,)),
             pltpu.SemaphoreType.DMA((3, NEAR)),
             pltpu.SemaphoreType.DMA((3, NEAR)),
             pltpu.SemaphoreType.DMA((3, FAR)),
             pltpu.SemaphoreType.DMA((3, FAR)),
         ],
-        compiler_params=pltpu.CompilerParams(collective_id=1, has_side_effects=True),
-        name="tail",
-    )(logits, offset, divisor[:, None], softening[:, None], share[None, :])
+        compiler_params=pltpu.CompilerParams(
+            collective_id=1, has_side_effects=True, vmem_limit_bytes=56 * 2**20
+        ),
+        name="step",
+    )(latent, weights, offset, divisor[:, None], softening[:, None], share[None, :])
 
 
 def per_device(
@@ -254,16 +443,17 @@
         additive_offset_table.astype(jnp.float32)
         - recurrence_charge[:, None] * count_float
         - appearance_charge[:, None] * (occurrence_tally > 0).astype(jnp.float32)
-    ).astype(jnp.bfloat16)
-    relaid = lax.all_to_all(offset, VOCAB, split_axis=1, concat_axis=0, tiled=True)
-    partial_logits = jnp.dot(
-        gather_axes(latent_vector, (("vocab_0", "vocab_1", "vocab_2"), "vocab_3"), 0),
+    )
+    rows = recurrence_divisor.shape[0]
+    offset = lax.reduce_precision(offset, 8, 7).reshape(2, FAR, 8, -1, 128)
+    out, cutoff = step(
+        latent_vector,
         unembedding_matrix,
-        preferred_element_type=jnp.float32,
-    )
-    logits = sum_at_owner(partial_logits, "seq")
-    out, cutoff = tail(
-        logits, relaid, recurrence_divisor, softening_divisor, nucleus_share_limit
+        offset,
+        recurrence_divisor,
+        softening_divisor,
+        nucleus_share_limit,
+        rows,
     )
     return out, cutoff.reshape(-1)
 

time: 168 us -> 130 us (0.77)
  Pallas kernels: 54.8 us -> 119 us
  waiting for transfers between devices: 48.9 us -> 0 us
  starting transfers between devices: 29.7 us -> 0 us
  blocking collectives: 8.87 us -> 0 us
  local copies, waits for them, and re-layouts: 13.9 us -> 5.62 us
  matrix products: 5.44 us -> 0 us
    pallas_call x1, Pallas kernels: 54.8 us -> 119 us  [step(): pl.pallas_call(step_kernel, out_shape=(jax.ShapeDtypeStruct((rows, column...]
    all_to_all x3 -> x0, waiting for transfers between devices: 48.9 us -> none  [the longest x1 30.5 us: sum_at_owner(): lax.all_to_all(tiles, axis, split_axis=0, concat_axis=0, tiled=True)]
    all_to_all x3 -> x0, starting transfers between devices: 29.7 us -> none  [the longest x1 15.3 us: sent_to_all(): lax.all_to_all(jnp.broadcast_to(array[None], (count, *array.shape)), axis...]
    all_to_all x1 -> x0, blocking collectives: 8.87 us -> none  [sent_to_all(): lax.all_to_all(jnp.broadcast_to(array[None], (count, *array.shape)), axis...]
    dot_general x1 -> x0, matrix products: 5.44 us -> none  [per_device(): jnp.dot(gather_axes(latent_vector, (('vocab_0', 'vocab_1', 'vocab_2'), 'v...]
    reduce_precision x0 -> x1, other arithmetic: none -> 3.23 us  [per_device(): offset = lax.reduce_precision(offset, 8, 7).reshape(2, FAR, 8, -1, 128)]
    dot_general x1 -> x0, local copies, waits for them, and re-layouts: 2.93 us -> none  [per_device(): jnp.dot(gather_axes(latent_vector, (('vocab_0', 'vocab_1', 'vocab_2'), 'v...]
    unnamed x14 -> x2, local copies, waits for them, and re-layouts: 5.19 us -> 2.84 us
  transfers between devices with their start and end apart: 3 -> 0, of which waited for: 3 -> 0; matrix products, arithmetic and copies ran while one was open for 10% -> 0% of each run, Pallas kernels for 0% -> 0%
where the time goes in v2:
time: 130 us
  Pallas kernels  119 us (92%)
  local copies, waits for them, and re-layouts  5.62 us (4%)
  other arithmetic  3.23 us (2%)
  between operations  1.93 us (1%)
    pallas_call x1, Pallas kernels, step(): pl.pallas_call(step_kernel, out_shape=(jax.ShapeDtypeStruct((rows, column...  119 us
    reduce_precision x1, other arithmetic, per_device(): offset = lax.reduce_precision(offset, 8, 7).reshape(2, FAR, 8, -1, 128)  3.23 us
    unnamed x2, local copies, waits for them, and re-layouts  2.84 us

profile of v2, /device:TPU:1, one launch (start us, length us, event | category | flops | bytes accessed | tf_op | source)
XLA Modules:
  0.0 130.1 jit_solution(12239134844576208572)
XLA Ops:
  1.9 1.4 %copy.11.divisor = f32[128,1]{1,0:T(8,128)} copy(f32[128,1]{0,1:T(1,128)} %bitcast.10) | data formatting | bytes 1024 | tf_op jit(solution)/shard_map/broadcast_in_dim | solution.py:427
  3.3 1.4 %copy.12.softening = f32[128,1]{1,0:T(8,128)} copy(f32[128,1]{0,1:T(1,128)} %bitcast.11) | data formatting | bytes 1024 | tf_op jit(solution)/shard_map/broadcast_in_dim | solution.py:427
  4.7 3.2 %fusion.1 = f32[1,131072]{1,0:T(1,128)} fusion(s32[1,131072]{1,0:T(1,128)} %param.11, bf16[1,131072]{1,0:T(2,128)(2,1)} %param.12, f32[]{:T(128)} %bitcast.8, f32[]{:T(128)} %bitcast.7), kind=kLoop, calls=%fused_computation.2 | loop fusion | flops 1048576 | bytes 1310728 | tf_op jit(solution)/shard_map/reduce_precision | solution.py:448
  7.9 119.3 %step.1 = (bf16[128,1024]{1,0:T(8,128)(2,1)}, f32[1,128]{1,0:T(1,128)}) custom-call(bf16[4,1792]{1,0:T(4,128)(2,1)} %latent.1, bf16[1792,1024]{1,0:T(8,128)(2,1)} %weights_hbm.1, f32[2,8,8,8,128]{4,3,2,1,0:T(8,128)} %bitcast.9, f32[128,1]{1,0:T(8,128)} %copy.11.divisor, f32[128,1]{1,0:T(8,128)} %copy.12.softening, f32[1,128]{1,0:T(1,128)} %bitcast.12), custom_call_target="tpu_custom_call" | custom-call | tf_op jit(solution)/shard_map/step/pallas_call | solution.py:389
  127.3 1.7 %copy.17 = bf16[128,1024]{1,0:T(8,128)(2,1)} copy(bf16[128,1024]{1,0:T(8,128)(2,1)} %get-tuple-element.8) | data formatting | bytes 524288
  128.9 1.2 copy.18

commit v3 on v2

--- a/solution.py
+++ b/solution.py
@@ -16,7 +16,8 @@
 LEVELS = (31, 15)
 SPAN = 32.0
 PARTS = 4
-COPIES = 96
+GROUP = 32
+COPIES = 112
 
 
 def near_index():
@@ -31,6 +32,14 @@
     return {
         "vocab_0": index // 8,
         "vocab_2": lax.rem(index // 2, 4),
+        "vocab_3": lax.rem(index, 2),
+    }
+
+
+def group_peer(index):
+    return {
+        "vocab_0": index // 16,
+        "vocab_1": lax.rem(index // 2, 8),
         "vocab_3": lax.rem(index, 2),
     }
 
@@ -101,13 +110,17 @@
 def step_kernel(
     latent,
     weights_hbm,
-    offset,
+    tally,
+    table,
+    charge,
+    appearance,
     divisor,
     softening,
     share,
     out,
     cutoff,
     weights,
+    offset,
     few,
     hidden,
     partial,
@@ -147,10 +160,11 @@
     def greet(peer):
         pl.semaphore_signal(barrier, inc=1, device_id=peer, device_id_type=MESH)
 
+    group = (y * FAR + z) * 2 + core
+    for step in range(1, GROUP):
+        greet(group_peer(lax.rem(group + step, GROUP)))
     for step in range(1, NEAR):
         greet(near_peer(lax.rem(here + step, NEAR)))
-    for step in range(1, FAR):
-        greet(far_peer(lax.rem(z + step, FAR)))
     after, before = {"seq": lax.rem(seq + 1, 4)}, {"seq": lax.rem(seq + 3, 4)}
     greet(after)
     greet(before)
@@ -181,65 +195,115 @@
     def my_half(which):
         return pl.ds(pl.multiple_of(which * half, 128), half)
 
-    few[pair] = latent[:, my_half(core)]
-    pl.semaphore_wait(barrier, NEAR + FAR)
-
-    def pair_peer(index):
-        return {"vocab_2": index // 2, "vocab_3": lax.rem(index, 2)}
-
-    order = [4, 5, 3, 1, 2, 6, 7]
-    swaps = {}
-    for step in order:
-        there = lax.rem(pair + step, 8)
-        swaps[step] = send(
-            latent.at[:, my_half(lax.rem(there, 2))], few.at[pair], pair_peer(there)
-        )
-    for step in order:
-        source = lax.rem(pair + 8 - step, 8)
-        arrive(swaps[step], few.at[source], pair_peer(source))
-    joined = jnp.concatenate([few[k].astype(jnp.float32) for k in range(8)])
-
-    def block(which_y, which_z):
-        at = pl.multiple_of((which_y * FAR + which_z) * 32, 32)
-        return hidden.at[core, pl.ds(at, 32)]
-
-    hidden[core, pl.ds(pl.multiple_of((y * FAR + z) * 32, 32), 32)] = joined.astype(
-        jnp.bfloat16
-    )
-
-    other_core, other_y = {"vocab_3": 1 - core}, {"vocab_0": 1 - y}
-    up, down = {"vocab_1": lax.rem(z + 1, FAR)}, {"vocab_1": lax.rem(z + 7, FAR)}
-    shares = []
-
-    def to_core(which_y, which_z):
-        number = send(block(which_y, which_z), block(which_y, which_z), other_core)
-        at = pl.multiple_of((which_y * FAR + which_z) * 32, 32)
-        shares.append((number, hidden.at[1 - core, pl.ds(at, 32)]))
-
-    def pass_on(which_y, which_z, way):
-        piece = block(which_y, which_z)
-        return send(piece, piece, up if way == 0 else down)
-
-    ring = {}
-    mine = [y, 1 - y]
-    across = send(block(y, z), block(y, z), other_y)
-    for way in range(2):
-        ring[way, 0, 0] = pass_on(y, z, way)
-    arrive(across, block(1 - y, z), other_y)
-    for way in range(2):
-        ring[way, 0, 1] = pass_on(1 - y, z, way)
-    to_core(y, z)
-    to_core(1 - y, z)
-    for step in range(1, 5):
-        for k in range(2):
-            for way in range(2):
-                if step == 4 and way != k:
-                    continue
-                came = lax.rem(z + (8 - step if way == 0 else step), FAR)
-                arrive(ring[way, step - 1, k], block(mine[k], came), down if way == 0 else up)
-                if step < 3 or (step == 3 and way == k):
-                    ring[way, step, k] = pass_on(mine[k], came, way)
-                to_core(mine[k], came)
+    few[group] = latent[:, my_half(core)]
+    pl.semaphore_wait(barrier, NEAR + GROUP)
+
+    swaps = []
+    for step in range(1, GROUP):
+        there = lax.rem(group + step, GROUP)
+        swaps.append(
+            send(latent.at[:, my_half(lax.rem(there, 2))], few.at[group], group_peer(there))
+        )
+
+    flat = offset.reshape(tally.shape[0], 128)
+    lines = 64
+    each = jnp.broadcast_to(charge[...], (lines, 128))
+    once = jnp.broadcast_to(appearance[...], (lines, 128))
+
+    def shift_lines(k, carry):
+        base = pl.multiple_of(k * lines, lines)
+        line = table[:, pl.ds(pl.multiple_of(base * 128, lines * 128), lines * 128)]
+        line = line.astype(jnp.float32)
+        for j in range(lines):
+            flat[pl.ds(base + j, 1), :] = line[:, j * 128 : (j + 1) * 128]
+        at = pl.ds(base, lines)
+        count = tally[at, :].astype(jnp.float32)
+        value = (
+            flat[at, :] - each * count - once * jnp.where(count > 0, 1.0, 0.0)
+        )
+        flat[at, :] = value.astype(jnp.bfloat16).astype(jnp.float32)
+        return carry
+
+    lax.fori_loop(0, tally.shape[0] // lines, shift_lines, 0)
+
+    for step in range(1, GROUP):
+        source = lax.rem(group + GROUP - step, GROUP)
+        arrive(swaps[step - 1], few.at[source], group_peer(source))
+
+    other_core = {"vocab_3": 1 - core}
+    strip = rows // 4
+    targets = [lax.rem(seq + k, 4) for k in (2, 1, 3, 0)]
+
+    def block(side, which_x, target):
+        at = pl.multiple_of(target * strip, strip)
+        return hidden.at[side, which_x, pl.ds(at, strip)]
+
+    for k in range(4):
+        joined = [few[k * 8 + j].astype(jnp.float32) for j in range(8)]
+        hidden[core, x, pl.ds(k * strip, strip)] = jnp.concatenate(joined).astype(jnp.bfloat16)
+
+    shares, lines_sent = [[] for _ in targets], []
+
+    def to_core(k, which_x):
+        piece = block(core, which_x, targets[k])
+        shares[k].append((send(piece, piece, other_core), which_x))
+
+    for k, target in enumerate(targets):
+        piece = block(core, x, target)
+        lines_sent.append(
+            [
+                send(piece, piece, {"vocab_2": lax.rem(x + step, 4)})
+                for step in (2, 1, 3)
+            ]
+        )
+        to_core(k, x)
+
+    def ready(k):
+        for number, step in zip(lines_sent[k], (2, 1, 3)):
+            source = lax.rem(x + 4 - step, 4)
+            arrive(number, block(core, source, targets[k]), {"vocab_2": source})
+            to_core(k, source)
+        for number, which_x in shares[k]:
+            arrive(number, block(1 - core, which_x, targets[k]), other_core)
+
+    def multiply(slot, target):
+        at = pl.ds(pl.multiple_of(target * strip, strip), strip)
+        for k in range(PARTS):
+            cut = pl.ds(k * wide, wide)
+            total = jnp.dot(
+                hidden[0, :, at, :].reshape(rows, half),
+                weights[:half, cut],
+                preferred_element_type=jnp.float32,
+            ) + jnp.dot(
+                hidden[1, :, at, :].reshape(rows, half),
+                weights[half:, cut],
+                preferred_element_type=jnp.float32,
+            )
+            for i in range(4):
+                for j in range(4):
+                    partial[slot, pl.ds((j * 4 + i) * 8, 8), cut] = total[
+                        (i * 4 + j) * 8 : (i * 4 + j + 1) * 8
+                    ]
+            yield cut
+
+    first, last = pl.ds(0, mid), pl.ds(mid, mid)
+    relays = []
+    ready(0)
+    load.wait()
+    for k, cut in enumerate(multiply(0, targets[0])):
+        relays.append(
+            (
+                send(partial.at[0, first, cut], relay_in.at[0, :, cut], after),
+                send(partial.at[0, last, cut], relay_in.at[1, :, cut], before),
+            )
+        )
+    directs = []
+    ready(1)
+    for cut in multiply(1, targets[1]):
+        directs.append([send(partial.at[1, last, cut], direct_in.at[0, :, cut], after)])
+    ready(2)
+    for k, cut in enumerate(multiply(2, targets[2])):
+        directs[k].append(send(partial.at[2, first, cut], direct_in.at[1, :, cut], before))
 
     far_copies = []
     for step in range(1, FAR):
@@ -248,35 +312,6 @@
     own = pltpu.make_async_copy(offset.at[:, z], far_offset.at[z], local_sem.at[1])
     own.start()
 
-    load.wait()
-    for number, landing in shares:
-        arrive(number, landing, other_core)
-
-    def multiply(slot, target):
-        at = pl.ds(pl.multiple_of(target * rows, rows), rows)
-        for k in range(PARTS):
-            cut = pl.ds(k * wide, wide)
-            partial[slot, :, cut] = jnp.dot(
-                hidden[0, at, :], weights[:half, cut], preferred_element_type=jnp.float32
-            ) + jnp.dot(
-                hidden[1, at, :], weights[half:, cut], preferred_element_type=jnp.float32
-            )
-            yield cut
-
-    first, last = pl.ds(0, mid), pl.ds(mid, mid)
-    relays = []
-    for k, cut in enumerate(multiply(0, lax.rem(seq + 2, 4))):
-        relays.append(
-            (
-                send(partial.at[0, first, cut], relay_in.at[0, :, cut], after),
-                send(partial.at[0, last, cut], relay_in.at[1, :, cut], before),
-            )
-        )
-    directs = []
-    for cut in multiply(1, lax.rem(seq + 1, 4)):
-        directs.append([send(partial.at[1, last, cut], direct_in.at[0, :, cut], after)])
-    for k, cut in enumerate(multiply(2, lax.rem(seq + 3, 4))):
-        directs[k].append(send(partial.at[2, first, cut], direct_in.at[1, :, cut], before))
     finals = []
     for k in range(PARTS):
         cut = pl.ds(k * wide, wide)
@@ -286,7 +321,8 @@
         arrive(relays[k][1], relay_in.at[1, :, cut], after)
         partial[2, last, cut] += relay_in[1, :, cut]
         finals.append((one, send(partial.at[2, last, cut], final_in.at[1, :, cut], before)))
-    for cut in multiply(3, seq):
+    ready(3)
+    for cut in multiply(3, targets[3]):
         pass
 
     own.wait()
@@ -312,8 +348,9 @@
         source = lax.rem(here + NEAR - step, NEAR)
         arrive(near_copies[step - 1], landed(source), near_peer(source))
 
-    inverse = 1.0 / divisor[...]
-    cooler = 1.0 / softening[...]
+    factor = jnp.broadcast_to(divisor[...], (128, rows)).T
+    inverse = 1.0 / factor
+    cooler = 1.0 / jnp.broadcast_to(softening[...], (128, rows)).T
     highest = None
     for k in range(PARTS):
         cut = pl.ds(k * wide, wide)
@@ -327,7 +364,7 @@
             lower = partial[3, last, at] + (final_in[1, :, at] + direct_in[0, :, at])
             raw = jnp.concatenate([upper, lower])
             shift = near_offset[:, :, :, j, :].reshape(rows, 128)
-            scaled = jnp.where(raw > 0, raw * inverse, raw * divisor[...])
+            scaled = jnp.where(raw > 0, raw * inverse, raw * factor)
             changed = jnp.where(shift < 0, scaled, raw) + shift
             out[:, at] = changed.astype(jnp.bfloat16)
             turned = (changed * cooler).T
@@ -375,10 +412,15 @@
         copy.wait_send()
 
 
-def step(latent, weights, offset, divisor, softening, share, rows):
-    columns = weights.shape[1]
+def settle_kernel(out, cutoff, out_kept, cutoff_kept):
+    out_kept[...] = out[...]
+    cutoff_kept[...] = cutoff[...]
+
+
+def step(latent, weights, tally, table, charge, appearance, *by_row):
+    depth, columns = weights.shape
+    rows = by_row[0].shape[0]
     vmem = pl.BlockSpec(memory_space=pltpu.VMEM)
-    depth = weights.shape[0]
 
     def held(count, lines):
         return pltpu.VMEM((count, lines, 128), jnp.float32)
@@ -386,18 +428,20 @@
     def whole(*shape):
         return pltpu.VMEM(shape, jnp.float32)
 
-    return pl.pallas_call(
+    results = (
+        jax.ShapeDtypeStruct((rows, columns), jnp.bfloat16),
+        jax.ShapeDtypeStruct((1, rows), jnp.float32),
+    )
+    found = pl.pallas_call(
         step_kernel,
-        out_shape=(
-            jax.ShapeDtypeStruct((rows, columns), jnp.bfloat16),
-            jax.ShapeDtypeStruct((1, rows), jnp.float32),
-        ),
-        in_specs=[vmem, pl.BlockSpec(memory_space=pl.ANY)] + [vmem] * 4,
+        out_shape=results,
+        in_specs=[vmem, pl.BlockSpec(memory_space=pl.ANY)] + [vmem] * 7,
         out_specs=(vmem, vmem),
         scratch_shapes=[
             pltpu.VMEM((depth, columns), weights.dtype),
-            pltpu.VMEM((8, latent.shape[0], depth // 2), latent.dtype),
-            pltpu.VMEM((2, 4 * rows, depth // 2), latent.dtype),
+            whole(2, FAR, 8, columns // 128, 128),
+            pltpu.VMEM((GROUP, latent.shape[0], depth // 2), latent.dtype),
+            pltpu.VMEM((2, 4, rows, depth // 2), latent.dtype),
             whole(4, rows, columns),
             whole(2, rows // 2, columns),
             whole(2, rows // 2, columns),
@@ -424,37 +468,26 @@
             collective_id=1, has_side_effects=True, vmem_limit_bytes=56 * 2**20
         ),
         name="step",
-    )(latent, weights, offset, divisor[:, None], softening[:, None], share[None, :])
-
-
-def per_device(
-    latent_vector,
-    unembedding_matrix,
-    occurrence_tally,
-    additive_offset_table,
-    recurrence_charge,
-    appearance_charge,
-    recurrence_divisor,
-    softening_divisor,
-    nucleus_share_limit,
-):
-    count_float = occurrence_tally.astype(jnp.float32)
-    offset = (
-        additive_offset_table.astype(jnp.float32)
-        - recurrence_charge[:, None] * count_float
-        - appearance_charge[:, None] * (occurrence_tally > 0).astype(jnp.float32)
+    )(
+        latent,
+        weights,
+        tally.reshape(-1, 128),
+        table,
+        charge[None, :],
+        appearance[None, :],
+        *(part[None, :] for part in by_row),
     )
-    rows = recurrence_divisor.shape[0]
-    offset = lax.reduce_precision(offset, 8, 7).reshape(2, FAR, 8, -1, 128)
-    out, cutoff = step(
-        latent_vector,
-        unembedding_matrix,
-        offset,
-        recurrence_divisor,
-        softening_divisor,
-        nucleus_share_limit,
-        rows,
-    )
+    return pl.pallas_call(
+        settle_kernel,
+        out_shape=results,
+        in_specs=[vmem, vmem],
+        out_specs=(vmem, vmem),
+        name="settle",
+    )(*found)
+
+
+def per_device(*arguments):
+    out, cutoff = step(*arguments)
     return out, cutoff.reshape(-1)
 
 

time: 130 us -> 116 us (0.89)
  Pallas kernels: 119 us -> 113 us
  local copies, waits for them, and re-layouts: 5.62 us -> 0 us
  other arithmetic: 3.23 us -> 0 us
    pallas_call x1 -> x2, Pallas kernels: 119 us -> 113 us  [the longest x1 112 us: step(): pl.pallas_call(step_kernel, out_shape=results, in_specs=[vmem, pl.BlockSp...]
    reduce_precision x1 -> x0, other arithmetic: 3.23 us -> none  [per_device(): offset = lax.reduce_precision(offset, 8, 7).reshape(2, FAR, 8, -1, 128)]
    unnamed x2 -> x0, local copies, waits for them, and re-layouts: 2.84 us -> none
    broadcast_in_dim x2 -> x0, local copies, waits for them, and re-layouts: 2.78 us -> none  [the longest x1 1.39 us: step(): divisor[:, None]]
where the time goes in v3:
time: 116 us; the launch traced here: 115 us
  Pallas kernels  113 us (97%)
  between operations  1.93 us (2%)
    pallas_call x1, Pallas kernels, step(): pl.pallas_call(step_kernel, out_shape=results, in_specs=[vmem, pl.BlockSp...  112 us

profile of v3, /device:TPU:1, one launch (start us, length us, event | category | flops | bytes accessed | tf_op | source)
XLA Modules:
  0.0 115.4 jit_solution(17870114589507862593)
XLA Ops:
  1.9 111.8 %step.1 = (bf16[128,1024]{1,0:T(8,128)(2,1)}, f32[1,128]{1,0:T(1,128)}) custom-call(bf16[4,1792]{1,0:T(4,128)(2,1)} %latent.1, bf16[1792,1024]{1,0:T(8,128)(2,1)} %weights_hbm.1, s32[1024,128]{1,0:T(8,128)} %bitcast.9, bf16[1,131072]{1,0:T(2,128)(2,1)} %table.1, f32[1,1]{1,0:T(1,128)} %bitcast.7.charge, f32[1,1]{1,0:T(1,128)} %bitcast.8.appearance, ...), custom_call_target="tpu_custom_call" | custom-call | tf_op jit(solution)/shard_map/step/pallas_call | solution.py:435
  113.7 1.7 %settle.1 = (bf16[128,1024]{1,0:T(8,128)(2,1)}, f32[1,128]{1,0:T(1,128)}) custom-call(bf16[128,1024]{1,0:T(8,128)(2,1)} %get-tuple-element.6.out, f32[1,128]{1,0:T(1,128)} %get-tuple-element.7.cutoff), custom_call_target="tpu_custom_call" | custom-call | tf_op jit(solution)/shard_map/settle/pallas_call | solution.py:480

commit v4 on v3

--- a/solution.py
+++ b/solution.py
@@ -18,6 +18,7 @@
 PARTS = 4
 GROUP = 32
 COPIES = 112
+LIMIT = 524280.0
 
 
 def near_index():
@@ -124,9 +125,12 @@
     few,
     hidden,
     partial,
+    coded,
     relay_in,
     direct_in,
     final_in,
+    scale_out,
+    scale_in,
     far_offset,
     near_offset,
     scores,
@@ -284,26 +288,79 @@
                     partial[slot, pl.ds((j * 4 + i) * 8, 8), cut] = total[
                         (i * 4 + j) * 8 : (i * 4 + j + 1) * 8
                     ]
-            yield cut
 
     first, last = pl.ds(0, mid), pl.ds(mid, mid)
+    def turn(tile):
+        return tile.T[0:1, :]
+
+    def spread(line):
+        return jnp.broadcast_to(line, (128, rows)).T
+
+    def peak(slot):
+        most = jnp.abs(partial[slot, :, pl.ds(0, 128)])
+        for k in range(1, columns // 128):
+            most = jnp.maximum(most, jnp.abs(partial[slot, :, pl.ds(k * 128, 128)]))
+        most = jnp.maximum(jnp.max(most, axis=1, keepdims=True), 1e-30)
+        return jnp.broadcast_to(most, (rows, 128))
+
+    def encode(box, cut, value, gain):
+        gain = jnp.concatenate([gain] * (value.shape[1] // 128), axis=1)
+        whole = jnp.round(value * gain).astype(jnp.int32)
+        coded[box, pl.ds(0, mid), cut] = (whole >> 4).astype(jnp.int16)
+        low = whole & 15
+        packed = low[:quarter]
+        for k in range(1, 4):
+            packed = packed | (low[k * quarter : (k + 1) * quarter] << (4 * k))
+        coded[box, pl.ds(mid, quarter), cut] = (packed - 32768).astype(jnp.int16)
+        return coded.at[box, :, cut]
+
+    def decode(box, cut, unit):
+        high = box[pl.ds(0, mid), cut].astype(jnp.int32)
+        packed = box[pl.ds(mid, quarter), cut].astype(jnp.int32) + 32768
+        low = jnp.concatenate([(packed >> (4 * k)) & 15 for k in range(4)])
+        value = ((high << 4) + low).astype(jnp.float32)
+        return value * jnp.concatenate([unit] * (value.shape[1] // 128), axis=1)
+
+    quarter = mid // 4
+    cuts = [pl.ds(k * wide, wide) for k in range(PARTS)]
     relays = []
     ready(0)
     load.wait()
-    for k, cut in enumerate(multiply(0, targets[0])):
-        relays.append(
-            (
-                send(partial.at[0, first, cut], relay_in.at[0, :, cut], after),
-                send(partial.at[0, last, cut], relay_in.at[1, :, cut], before),
-            )
-        )
+    multiply(0, targets[0])
+    peak_0 = peak(0)
+    gain = LIMIT / peak_0
+    scale_out[0] = turn(peak_0)
+    scale_up = send(scale_out.at[0], scale_in.at[0], after)
+    scale_down = send(scale_out.at[0], scale_in.at[1], before)
+    for cut in cuts:
+        one = encode(0, cut, partial[0, first, cut], gain[:mid])
+        one = send(one, relay_in.at[0, :, cut], after)
+        two = encode(1, cut, partial[0, last, cut], gain[mid:])
+        relays.append((one, send(two, relay_in.at[1, :, cut], before)))
+    ready(1)
+    multiply(1, targets[1])
+    peak_1 = peak(1)
+    gain = LIMIT / peak_1
     directs = []
-    ready(1)
-    for cut in multiply(1, targets[1]):
-        directs.append([send(partial.at[1, last, cut], direct_in.at[0, :, cut], after)])
+    for cut in cuts:
+        one = encode(2, cut, partial[1, last, cut], gain[mid:])
+        directs.append([send(one, direct_in.at[0, :, cut], after)])
     ready(2)
-    for k, cut in enumerate(multiply(2, targets[2])):
-        directs[k].append(send(partial.at[2, first, cut], direct_in.at[1, :, cut], before))
+    multiply(2, targets[2])
+    peak_2 = peak(2)
+    gain = LIMIT / peak_2
+    for k, cut in enumerate(cuts):
+        two = encode(3, cut, partial[2, first, cut], gain[:mid])
+        directs[k].append(send(two, direct_in.at[1, :, cut], before))
+
+    arrive(scale_up, scale_in.at[0], before)
+    arrive(scale_down, scale_in.at[1], after)
+    peak_up, peak_down = spread(scale_in[0])[:mid], spread(scale_in[1])[mid:]
+    bound_up, bound_down = peak_up + peak_1[:mid], peak_down + peak_2[mid:]
+    scale_out[1] = turn(jnp.concatenate([bound_up, peak_1[mid:]]))
+    scale_out[2] = turn(jnp.concatenate([peak_2[:mid], bound_down]))
+    scale_up = send(scale_out.at[1], scale_in.at[2], after)
+    scale_down = send(scale_out.at[2], scale_in.at[3], before)
 
     far_copies = []
     for step in range(1, FAR):
@@ -313,17 +370,18 @@
     own.start()
 
     finals = []
-    for k in range(PARTS):
-        cut = pl.ds(k * wide, wide)
+    gain_up, gain_down = LIMIT / bound_up, LIMIT / bound_down
+    unit_up, unit_down = peak_up * (1.0 / LIMIT), peak_down * (1.0 / LIMIT)
+    for k, cut in enumerate(cuts):
         arrive(relays[k][0], relay_in.at[0, :, cut], before)
-        partial[1, first, cut] += relay_in[0, :, cut]
-        one = send(partial.at[1, first, cut], final_in.at[0, :, cut], after)
+        value = partial[1, first, cut] + decode(relay_in.at[0], cut, unit_up)
+        one = send(encode(4, cut, value, gain_up), final_in.at[0, :, cut], after)
         arrive(relays[k][1], relay_in.at[1, :, cut], after)
-        partial[2, last, cut] += relay_in[1, :, cut]
-        finals.append((one, send(partial.at[2, last, cut], final_in.at[1, :, cut], before)))
+        value = partial[2, last, cut] + decode(relay_in.at[1], cut, unit_down)
+        two = send(encode(5, cut, value, gain_down), final_in.at[1, :, cut], before)
+        finals.append((one, two))
     ready(3)
-    for cut in multiply(3, targets[3]):
-        pass
+    multiply(3, targets[3])
 
     own.wait()
     for step in range(1, FAR):
@@ -348,20 +406,29 @@
         source = lax.rem(here + NEAR - step, NEAR)
         arrive(near_copies[step - 1], landed(source), near_peer(source))
 
-    factor = jnp.broadcast_to(divisor[...], (128, rows)).T
+    factor = spread(divisor[...])
     inverse = 1.0 / factor
-    cooler = 1.0 / jnp.broadcast_to(softening[...], (128, rows)).T
+    cooler = 1.0 / spread(softening[...])
+    arrive(scale_up, scale_in.at[2], before)
+    arrive(scale_down, scale_in.at[3], after)
+    unit_up = spread(scale_in[2]) * (1.0 / LIMIT)
+    unit_down = spread(scale_in[3]) * (1.0 / LIMIT)
     highest = None
-    for k in range(PARTS):
-        cut = pl.ds(k * wide, wide)
+    for k, cut in enumerate(cuts):
         arrive(directs[k][0], direct_in.at[0, :, cut], before)
         arrive(directs[k][1], direct_in.at[1, :, cut], after)
         arrive(finals[k][0], final_in.at[0, :, cut], before)
         arrive(finals[k][1], final_in.at[1, :, cut], after)
         for j in range(k * wide // 128, (k + 1) * wide // 128):
             at = pl.ds(j * 128, 128)
-            upper = partial[3, first, at] + (final_in[0, :, at] + direct_in[1, :, at])
-            lower = partial[3, last, at] + (final_in[1, :, at] + direct_in[0, :, at])
+            upper = partial[3, first, at] + (
+                decode(final_in.at[0], at, unit_up[:mid])
+                + decode(direct_in.at[1], at, unit_down[:mid])
+            )
+            lower = partial[3, last, at] + (
+                decode(final_in.at[1], at, unit_down[mid:])
+                + decode(direct_in.at[0], at, unit_up[mid:])
+            )
             raw = jnp.concatenate([upper, lower])
             shift = near_offset[:, :, :, j, :].reshape(rows, 128)
             scaled = jnp.where(raw > 0, raw * inverse, raw * factor)
@@ -427,6 +494,9 @@
 
     def whole(*shape):
         return pltpu.VMEM(shape, jnp.float32)
+
+    def boxes(count):
+        return pltpu.VMEM((count, rows * 5 // 8, columns), jnp.int16)
 
     results = (
         jax.ShapeDtypeStruct((rows, columns), jnp.bfloat16),
@@ -443,9 +513,12 @@
             pltpu.VMEM((GROUP, latent.shape[0], depth // 2), latent.dtype),
             pltpu.VMEM((2, 4, rows, depth // 2), latent.dtype),
             whole(4, rows, columns),
-            whole(2, rows // 2, columns),
-            whole(2, rows // 2, columns),
-            whole(2, rows // 2, columns),
+            boxes(6),
+            boxes(2),
+            boxes(2),
+            boxes(2),
+            whole(3, 1, 128),
+            whole(4, 1, 128),
             whole(FAR, 2, 8, columns // 128, 128),
             whole(2, FAR, 8, columns // 128, 128),
             whole(columns, rows),

time: 116 us -> 104 us (0.90)
  Pallas kernels: 113 us -> 102 us
    pallas_call x1, Pallas kernels: 112 us -> 101 us  [step(): pl.pallas_call(step_kernel, out_shape=results, in_specs=[vmem, pl.BlockSp...]
where the time goes in v4:
time: 104 us
  Pallas kernels  102 us (98%)
  between operations  1.93 us (2%)
    pallas_call x1, Pallas kernels, step(): pl.pallas_call(step_kernel, out_shape=results, in_specs=[vmem, pl.BlockSp...  101 us

profile of v4, /device:TPU:1, one launch (start us, length us, event | category | flops | bytes accessed | tf_op | source)
XLA Modules:
  0.0 104.1 jit_solution(14174556616078314311)
XLA Ops:
  1.9 100.5 %step.1 = (bf16[128,1024]{1,0:T(8,128)(2,1)}, f32[1,128]{1,0:T(1,128)}) custom-call(bf16[4,1792]{1,0:T(4,128)(2,1)} %latent.1, bf16[1792,1024]{1,0:T(8,128)(2,1)} %weights_hbm.1, s32[1024,128]{1,0:T(8,128)} %bitcast.9, bf16[1,131072]{1,0:T(2,128)(2,1)} %table.1, f32[1,1]{1,0:T(1,128)} %bitcast.7.charge, f32[1,1]{1,0:T(1,128)} %bitcast.8.appearance, ...), custom_call_target="tpu_custom_call" | custom-call | tf_op jit(solution)/shard_map/step/pallas_call | solution.py:505
  102.5 1.7 %settle.1 = (bf16[128,1024]{1,0:T(8,128)(2,1)}, f32[1,128]{1,0:T(1,128)}) custom-call(bf16[128,1024]{1,0:T(8,128)(2,1)} %get-tuple-element.6.out, f32[1,128]{1,0:T(1,128)} %get-tuple-element.7.cutoff), custom_call_target="tpu_custom_call" | custom-call | tf_op jit(solution)/shard_map/settle/pallas_call | solution.py:553

commit v5 on v4

--- a/solution.py
+++ b/solution.py
@@ -43,6 +43,10 @@
         "vocab_1": lax.rem(index // 2, 8),
         "vocab_3": lax.rem(index, 2),
     }
+
+
+def pair_peer(index):
+    return {"vocab_2": index // 2, "vocab_3": lax.rem(index, 2)}
 
 
 def far_peer(index):
@@ -131,8 +135,11 @@
     final_in,
     scale_out,
     scale_in,
+    offset_out,
+    offset_pair,
     far_offset,
     near_offset,
+    changed_out,
     scores,
     terms,
     near_a,
@@ -225,10 +232,14 @@
         value = (
             flat[at, :] - each * count - once * jnp.where(count > 0, 1.0, 0.0)
         )
-        flat[at, :] = value.astype(jnp.bfloat16).astype(jnp.float32)
+        flat[at, :] = value
         return carry
 
     lax.fori_loop(0, tally.shape[0] // lines, shift_lines, 0)
+    other_y = {"vocab_0": 1 - y}
+    offset_out[...] = offset[1 - y].astype(jnp.bfloat16)
+    offset_pair[y] = offset[y].astype(jnp.bfloat16)
+    crossing = send(offset_out, offset_pair.at[y], other_y)
 
     for step in range(1, GROUP):
         source = lax.rem(group + GROUP - step, GROUP)
@@ -261,6 +272,14 @@
             ]
         )
         to_core(k, x)
+
+    arrive(crossing, offset_pair.at[1 - y], other_y)
+    far_copies = []
+    for step in range(1, FAR):
+        there = lax.rem(z + step, FAR)
+        far_copies.append(send(offset_pair.at[:, there], far_offset.at[:, z], far_peer(there)))
+    own = pltpu.make_async_copy(offset_pair.at[:, z], far_offset.at[:, z], local_sem.at[1])
+    own.start()
 
     def ready(k):
         for number, step in zip(lines_sent[k], (2, 1, 3)):
@@ -362,11 +381,19 @@
     scale_up = send(scale_out.at[1], scale_in.at[2], after)
     scale_down = send(scale_out.at[2], scale_in.at[3], before)
 
-    far_copies = []
+    own.wait()
     for step in range(1, FAR):
-        there = lax.rem(z + step, FAR)
-        far_copies.append(send(offset.at[:, there], far_offset.at[z], far_peer(there)))
-    own = pltpu.make_async_copy(offset.at[:, z], far_offset.at[z], local_sem.at[1])
+        source = lax.rem(z + FAR - step, FAR)
+        arrive(far_copies[step - 1], far_offset.at[:, source], far_peer(source))
+    pair_copies = []
+    for step in range(1, 8):
+        there = lax.rem(pair + step, 8)
+        pair_copies.append(
+            send(far_offset.at[:, :, there], near_offset.at[:, :, pair], pair_peer(there))
+        )
+    own = pltpu.make_async_copy(
+        far_offset.at[:, :, pair], near_offset.at[:, :, pair], local_sem.at[2]
+    )
     own.start()
 
     finals = []
@@ -384,27 +411,10 @@
     multiply(3, targets[3])
 
     own.wait()
-    for step in range(1, FAR):
-        source = lax.rem(z + FAR - step, FAR)
-        arrive(far_copies[step - 1], far_offset.at[source], far_peer(source))
-
-    def landed(index):
-        return near_offset.at[index // 8, :, lax.rem(index, 8)]
-
-    near_copies = []
-    for step in range(1, NEAR):
-        there = lax.rem(here + step, NEAR)
-        near_copies.append(
-            send(
-                far_offset.at[:, there // 8, lax.rem(there, 8)], landed(here), near_peer(there)
-            )
-        )
-    own = pltpu.make_async_copy(far_offset.at[:, y, pair], landed(here), local_sem.at[2])
-    own.start()
-    own.wait()
-    for step in range(1, NEAR):
-        source = lax.rem(here + NEAR - step, NEAR)
-        arrive(near_copies[step - 1], landed(source), near_peer(source))
+    for step in range(1, 8):
+        source = lax.rem(pair + 8 - step, 8)
+        arrive(pair_copies[step - 1], near_offset.at[:, :, source], pair_peer(source))
+    offset[...] = near_offset[...].astype(jnp.float32)
 
     factor = spread(divisor[...])
     inverse = 1.0 / factor
@@ -430,10 +440,10 @@
                 + decode(direct_in.at[0], at, unit_up[mid:])
             )
             raw = jnp.concatenate([upper, lower])
-            shift = near_offset[:, :, :, j, :].reshape(rows, 128)
+            shift = offset[:, :, :, j, :].reshape(rows, 128)
             scaled = jnp.where(raw > 0, raw * inverse, raw * factor)
             changed = jnp.where(shift < 0, scaled, raw) + shift
-            out[:, at] = changed.astype(jnp.bfloat16)
+            changed_out[:, at] = changed.astype(jnp.bfloat16)
             turned = (changed * cooler).T
             scores[at, :] = turned
             most = jnp.max(turned, axis=0, keepdims=True)
@@ -447,6 +457,8 @@
             sem_far_recv.at[turn],
         )
 
+    leave = pltpu.make_async_copy(changed_out, out, local_sem.at[3])
+    leave.start()
     largest, more = reduced(highest, near_a, far_a, sems(0), jnp.maximum)
     sent += more
     total = jnp.zeros((8, 128), jnp.float32)
@@ -475,6 +487,7 @@
     below = jnp.where(sums[: LEVELS[1]] < target, 1.0, 0.0)
     lower = lower + jnp.sum(below, axis=0, keepdims=True)
     cutoff[...] = largest - unit * (lower + 1.0)
+    leave.wait()
     for copy in sent:
         copy.wait_send()
 
@@ -506,7 +519,7 @@
         step_kernel,
         out_shape=results,
         in_specs=[vmem, pl.BlockSpec(memory_space=pl.ANY)] + [vmem] * 7,
-        out_specs=(vmem, vmem),
+        out_specs=(pl.BlockSpec(memory_space=pl.ANY), vmem),
         scratch_shapes=[
             pltpu.VMEM((depth, columns), weights.dtype),
             whole(2, FAR, 8, columns // 128, 128),
@@ -519,8 +532,11 @@
             boxes(2),
             whole(3, 1, 128),
             whole(4, 1, 128),
-            whole(FAR, 2, 8, columns // 128, 128),
-            whole(2, FAR, 8, columns // 128, 128),
+            pltpu.VMEM((FAR, 8, columns // 128, 128), jnp.bfloat16),
+            pltpu.VMEM((2, FAR, 8, columns // 128, 128), jnp.bfloat16),
+            pltpu.VMEM((2, FAR, 8, columns // 128, 128), jnp.bfloat16),
+            pltpu.VMEM((2, FAR, 8, columns // 128, 128), jnp.bfloat16),
+            pltpu.VMEM((rows, columns), jnp.bfloat16),
             whole(columns, rows),
             whole(columns, rows),
             held(NEAR, 1),
@@ -531,7 +547,7 @@
             held(FAR, LEVELS[1] + 1),
             pltpu.SemaphoreType.DMA((COPIES,)),
             pltpu.SemaphoreType.DMA((COPIES,)),
-            pltpu.SemaphoreType.DMA((3,)),
+            pltpu.SemaphoreType.DMA((4,)),
             pltpu.SemaphoreType.DMA((3, NEAR)),
             pltpu.SemaphoreType.DMA((3, NEAR)),
             pltpu.SemaphoreType.DMA((3, FAR)),

time: 104 us -> 94.9 us (0.913)
  Pallas kernels: 102 us -> 92.8 us
    pallas_call x1, Pallas kernels: 101 us -> 91.2 us  [step(): pl.pallas_call(step_kernel, out_shape=results, in_specs=[vmem, pl.BlockSp...]
where the time goes in v5:
time: 94.9 us; the launch traced here: 94.8 us
  Pallas kernels  92.8 us (98%)
  between operations  1.93 us (2%)
    pallas_call x1, Pallas kernels, step(): pl.pallas_call(step_kernel, out_shape=results, in_specs=[vmem, pl.BlockSp...  91.2 us

profile of v5, /device:TPU:1, one launch (start us, length us, event | category | flops | bytes accessed | tf_op | source)
XLA Modules:
  0.0 94.8 jit_solution(13147628051051803166)
XLA Ops:
  1.9 91.2 %step.1 = (bf16[128,1024]{1,0:T(8,128)(2,1)}, f32[1,128]{1,0:T(1,128)}) custom-call(bf16[4,1792]{1,0:T(4,128)(2,1)} %latent.1, bf16[1792,1024]{1,0:T(8,128)(2,1)} %weights_hbm.1, s32[1024,128]{1,0:T(8,128)} %bitcast.9, bf16[1,131072]{1,0:T(2,128)(2,1)} %table.1, f32[1,1]{1,0:T(1,128)} %bitcast.7.charge, f32[1,1]{1,0:T(1,128)} %bitcast.8.appearance, ...), custom_call_target="tpu_custom_call" | custom-call | tf_op jit(solution)/shard_map/step/pallas_call | solution.py:518
  93.1 1.7 %settle.1 = (bf16[128,1024]{1,0:T(8,128)(2,1)}, f32[1,128]{1,0:T(1,128)}) custom-call(bf16[128,1024]{1,0:T(8,128)(2,1)} %get-tuple-element.6.out, f32[1,128]{1,0:T(1,128)} %get-tuple-element.7.cutoff), custom_call_target="tpu_custom_call" | custom-call | tf_op jit(solution)/shard_map/settle/pallas_call | solution.py:569

commit v6 on v5

--- a/solution.py
+++ b/solution.py
@@ -1,3 +1,4 @@
+import functools
 import itertools
 
 import jax
@@ -14,6 +15,7 @@
 NEAR = 16
 FAR = 8
 LEVELS = (31, 15)
+SPLIT = (2, 2)
 SPAN = 32.0
 PARTS = 4
 GROUP = 32
@@ -53,20 +55,31 @@
     return {"vocab_1": index}
 
 
-def exchange(held, me, count, peer, send_sem, recv_sem):
+def near_distance(step):
+    return (step // 8) + min(step // 2 % 4, 4 - step // 2 % 4)
+
+
+def far_distance(step):
+    return min(step, FAR - step)
+
+
+def begin(held, me, count, peer, distance, send_sem, recv_sem):
     copies = []
-    for step in range(1, count):
-        there = lax.rem(me + step, count)
+    for step in sorted(range(1, count), key=lambda k: -distance(k)):
         copy = pltpu.make_async_remote_copy(
             src_ref=held.at[me],
             dst_ref=held.at[me],
             send_sem=send_sem.at[step],
             recv_sem=recv_sem.at[step],
-            device_id=peer(there),
+            device_id=peer(lax.rem(me + step, count)),
             device_id_type=MESH,
         )
         copy.start()
         copies.append(copy)
+    return copies
+
+
+def finish(held, me, count, peer, distance, send_sem, recv_sem, combine):
     for step in range(1, count):
         source = lax.rem(me + count - step, count)
         pltpu.make_async_remote_copy(
@@ -77,22 +90,31 @@
             device_id=peer(source),
             device_id_type=MESH,
         ).wait_recv()
-    return copies
-
-
-def reduced(values, near, far, sems, combine):
+    whole = held[0]
+    for k in range(1, count):
+        whole = combine(whole, held[k])
+    return whole
+
+
+def reduced(parts, near, far, sems, combine):
     here, there = near_index(), lax.axis_index("vocab_1")
-    near[here] = values
-    sent = exchange(near, here, NEAR, near_peer, sems[0], sems[1])
-    part = near[0]
-    for k in range(1, NEAR):
-        part = combine(part, near[k])
-    far[there] = part
-    sent += exchange(far, there, FAR, far_peer, sems[2], sems[3])
-    whole = far[0]
-    for k in range(1, FAR):
-        whole = combine(whole, far[k])
-    return whole, sent
+    sent, wholes = [], []
+    ways = [
+        (
+            (near.at[k], here, NEAR, near_peer, near_distance, sems[0].at[k], sems[1].at[k]),
+            (far.at[k], there, FAR, far_peer, far_distance, sems[2].at[k], sems[3].at[k]),
+        )
+        for k in range(len(parts))
+    ]
+    for k, part in enumerate(parts):
+        near[k, here] = part()
+        sent += begin(*ways[k][0])
+    for k in range(len(parts)):
+        far[k, there] = finish(*ways[k][0], combine)
+        sent += begin(*ways[k][1])
+    for k in range(len(parts)):
+        wholes.append(finish(*ways[k][1], combine))
+    return jnp.concatenate(wholes), sent
 
 
 def masses(scores, weights, limits):
@@ -151,10 +173,7 @@
     send_sem,
     recv_sem,
     local_sem,
-    sem_near_send,
-    sem_near_recv,
-    sem_far_send,
-    sem_far_recv,
+    *round_sems,
 ):
     y, z = lax.axis_index("vocab_0"), lax.axis_index("vocab_1")
     x, core = lax.axis_index("vocab_2"), lax.axis_index("vocab_3")
@@ -209,11 +228,11 @@
     few[group] = latent[:, my_half(core)]
     pl.semaphore_wait(barrier, NEAR + GROUP)
 
-    swaps = []
-    for step in range(1, GROUP):
+    swaps = {}
+    for step in sorted(range(1, GROUP), key=lambda k: -min(k // 2 % 8, 8 - k // 2 % 8)):
         there = lax.rem(group + step, GROUP)
-        swaps.append(
-            send(latent.at[:, my_half(lax.rem(there, 2))], few.at[group], group_peer(there))
+        swaps[step] = send(
+            latent.at[:, my_half(lax.rem(there, 2))], few.at[group], group_peer(there)
         )
 
     flat = offset.reshape(tally.shape[0], 128)
@@ -243,7 +262,7 @@
 
     for step in range(1, GROUP):
         source = lax.rem(group + GROUP - step, GROUP)
-        arrive(swaps[step - 1], few.at[source], group_peer(source))
+        arrive(swaps[step], few.at[source], group_peer(source))
 
     other_core = {"vocab_3": 1 - core}
     strip = rows // 4
@@ -449,17 +468,10 @@
             most = jnp.max(turned, axis=0, keepdims=True)
             highest = most if highest is None else jnp.maximum(highest, most)
 
-    def sems(turn):
-        return (
-            sem_near_send.at[turn],
-            sem_near_recv.at[turn],
-            sem_far_send.at[turn],
-            sem_far_recv.at[turn],
-        )
-
+    sems = [round_sems[4 * k : 4 * k + 4] for k in range(3)]
     leave = pltpu.make_async_copy(changed_out, out, local_sem.at[3])
     leave.start()
-    largest, more = reduced(highest, near_a, far_a, sems(0), jnp.maximum)
+    largest, more = reduced([lambda: highest], near_a, far_a, sems[0], jnp.maximum)
     sent += more
     total = jnp.zeros((8, 128), jnp.float32)
     chunk = 64
@@ -470,8 +482,17 @@
         total = total + jnp.sum(grown.reshape(chunk // 8, 8, 128), axis=0)
 
     first = [largest - (SPAN / (LEVELS[0] + 1)) * (k + 1) for k in range(LEVELS[0])]
-    rows = [jnp.sum(total, axis=0, keepdims=True)] + masses(scores, terms, first)
-    sums, more = reduced(jnp.concatenate(rows), near_b, far_b, sems(1), jnp.add)
+    total = jnp.sum(total, axis=0, keepdims=True)
+
+    def cut_masses(limits, lead=None):
+        found = masses(scores, terms, limits)
+        return jnp.concatenate(found if lead is None else [lead] + found)
+
+    depth = (LEVELS[0] + 1) // SPLIT[0]
+    parts = [functools.partial(cut_masses, first[: depth - 1], total)]
+    for k in range(1, SPLIT[0]):
+        parts.append(functools.partial(cut_masses, first[k * depth - 1 : (k + 1) * depth - 1]))
+    sums, more = reduced(parts, near_b, far_b, sems[1], jnp.add)
     sent += more
     target = share[...] * sums[0:1]
     lower = jnp.sum(
@@ -480,9 +501,13 @@
 
     unit = SPAN / ((LEVELS[0] + 1) * (LEVELS[1] + 1))
     second = [largest - unit * (lower + (k + 1)) for k in range(LEVELS[1])]
-    rows = masses(scores, terms, second)
-    rows.append(rows[-1])
-    sums, more = reduced(jnp.concatenate(rows), near_c, far_c, sems(2), jnp.add)
+    depth = (LEVELS[1] + 1) // SPLIT[1]
+    second.append(second[-1])
+    parts = [
+        functools.partial(cut_masses, second[k * depth : (k + 1) * depth])
+        for k in range(SPLIT[1])
+    ]
+    sums, more = reduced(parts, near_c, far_c, sems[2], jnp.add)
     sent += more
     below = jnp.where(sums[: LEVELS[1]] < target, 1.0, 0.0)
     lower = lower + jnp.sum(below, axis=0, keepdims=True)
@@ -502,8 +527,8 @@
     rows = by_row[0].shape[0]
     vmem = pl.BlockSpec(memory_space=pltpu.VMEM)
 
-    def held(count, lines):
-        return pltpu.VMEM((count, lines, 128), jnp.float32)
+    def held(split, count, lines):
+        return pltpu.VMEM((split, count, lines, 128), jnp.float32)
 
     def whole(*shape):
         return pltpu.VMEM(shape, jnp.float32)
@@ -539,19 +564,20 @@
             pltpu.VMEM((rows, columns), jnp.bfloat16),
             whole(columns, rows),
             whole(columns, rows),
-            held(NEAR, 1),
-            held(FAR, 1),
-            held(NEAR, LEVELS[0] + 1),
-            held(FAR, LEVELS[0] + 1),
-            held(NEAR, LEVELS[1] + 1),
-            held(FAR, LEVELS[1] + 1),
+            held(1, NEAR, 1),
+            held(1, FAR, 1),
+            held(SPLIT[0], NEAR, (LEVELS[0] + 1) // SPLIT[0]),
+            held(SPLIT[0], FAR, (LEVELS[0] + 1) // SPLIT[0]),
+            held(SPLIT[1], NEAR, (LEVELS[1] + 1) // SPLIT[1]),
+            held(SPLIT[1], FAR, (LEVELS[1] + 1) // SPLIT[1]),
             pltpu.SemaphoreType.DMA((COPIES,)),
             pltpu.SemaphoreType.DMA((COPIES,)),
             pltpu.SemaphoreType.DMA((4,)),
-            pltpu.SemaphoreType.DMA((3, NEAR)),
-            pltpu.SemaphoreType.DMA((3, NEAR)),
-            pltpu.SemaphoreType.DMA((3, FAR)),
-            pltpu.SemaphoreType.DMA((3, FAR)),
+        ]
+        + [
+            pltpu.SemaphoreType.DMA((split, count))
+            for split in (1, *SPLIT)
+            for count in (NEAR, NEAR, FAR, FAR)
         ],
         compiler_params=pltpu.CompilerParams(
             collective_id=1, has_side_effects=True, vmem_limit_bytes=56 * 2**20

time: 94.9 us -> 93.1 us (0.981)
  Pallas kernels: 92.8 us -> 90.9 us
    pallas_call x1, Pallas kernels: 91.2 us -> 89.3 us  [step(): pl.pallas_call(step_kernel, out_shape=results, in_specs=[vmem, pl.BlockSp...]
where the time goes in v6:
time: 93.1 us; the launch traced here: 92.9 us
  Pallas kernels  90.9 us (98%)
  between operations  1.93 us (2%)
    pallas_call x1, Pallas kernels, step(): pl.pallas_call(step_kernel, out_shape=results, in_specs=[vmem, pl.BlockSp...  89.3 us

profile of v6, /device:TPU:1, one launch (start us, length us, event | category | flops | bytes accessed | tf_op | source)
XLA Modules:
  0.0 92.9 jit_solution(18020096712010288577)
XLA Ops:
  1.9 89.3 %step.1 = (bf16[128,1024]{1,0:T(8,128)(2,1)}, f32[1,128]{1,0:T(1,128)}) custom-call(bf16[4,1792]{1,0:T(4,128)(2,1)} %latent.1, bf16[1792,1024]{1,0:T(8,128)(2,1)} %weights_hbm.1, s32[1024,128]{1,0:T(8,128)} %bitcast.9, bf16[1,131072]{1,0:T(2,128)(2,1)} %table.1, f32[1,1]{1,0:T(1,128)} %bitcast.7.charge, f32[1,1]{1,0:T(1,128)} %bitcast.8.appearance, ...), custom_call_target="tpu_custom_call" | custom-call | tf_op jit(solution)/shard_map/step/pallas_call | solution.py:543
  91.2 1.7 %settle.1 = (bf16[128,1024]{1,0:T(8,128)(2,1)}, f32[1,128]{1,0:T(1,128)}) custom-call(bf16[128,1024]{1,0:T(8,128)(2,1)} %get-tuple-element.6.out, f32[1,128]{1,0:T(1,128)} %get-tuple-element.7.cutoff), custom_call_target="tpu_custom_call" | custom-call | tf_op jit(solution)/shard_map/settle/pallas_call | solution.py:595
